TPU v7x, 128 devices: a whole 4x4x4 slice. The times are simulated.
128 devices in a mesh: line: 8 (over z, core), slab: 16 (over y, x).
Axes of the slice: x: 4, y: 4, z: 4, core: 2. Of those that a mesh axis runs over, the one named last changes fastest.
Arguments:
- mass_per_volume: float32 [4096, 2048], P('line', 'slab'), may hold values from 0.5 to 2
- fluid_speed_field: float32 [3, 4096, 2048], P(None, 'line', 'slab'), may hold values from -3 to 3
- fluid_thrust_field: float32 [4096, 2048], P('line', 'slab'), may hold values from 0.5 to 2
- shock_damping_field: float32 [4096, 2048], P('line', 'slab'), may hold values from 0.05 to 2
- grain_holding_processor: int32 [1048576, 1], P(('line', 'slab')), may hold values from 0 to 127; in each aligned block of 8192 rows (0 to 8191, 8192 to 16383, ...) at most 256 rows name the same one
- grain_mesh_slot: int32 [1048576], P(('line', 'slab')), may hold values from 0 to 65535
- grain_speed_vector: float32 [3, 1048576], P(None, ('line', 'slab')), may hold values from -3 to 3
- fluid_speed_at_grain: float32 [3, 1048576], P(None, ('line', 'slab')), may hold values from -3 to 3
- thermal_states: float32 [2, 1048576], P(None, ('line', 'slab')), may hold values from 0.5 to 2
- grain_mass_over_lag: float32 [1048576], P(('line', 'slab')), may hold values from 0.5 to 4
Outputs:
- gas_rate: float32 [5, 4096, 2048], P(None, 'line', 'slab')
Inputs may be any that keep to these rules, and one draw needn't show every extreme that they name: `grain_holding_processor`: within the rows of one device, each destination device is named at most 256 times, and in some device's rows some destination is named exactly 256 times.
All inputs are finite; a program needn't handle non-finite values.
Results may differ from a plain program's by a relative error of at most 0.0003.
Values sent between devices are 32-bit elements; how exact they have to be, the bound alone decides.
No kernel may reach another device: no remote copies, remote signals or barrier semaphores. Data moves between devices by JAX's collectives and lax.ppermute only.
A program may use at most 64 MiB of HBM per device.

v0:
```python
import functools

import jax
import jax.numpy as jnp
import numpy as np
from jax import lax
from jax.experimental import pallas as pl
from jax.experimental.pallas import tpu as pltpu
from jax.sharding import PartitionSpec as P

band_one = 0.5
band_two = 0.05
rhs_one = 17.0 / 12.0
rhs_two = 101.0 / 150.0
rhs_three = 0.01
gamma_gas = 1.4
adiabatic_exponent = 0.6
highest = lax.Precision.HIGHEST
f32 = jnp.float32
bf16 = jnp.bfloat16

HALVES = 2
GROUPS = 4
BUCKETS = HALVES * GROUPS
STEP = 4
CHUNK = 4


def operator_tables(cells):
    sums = np.roots([band_two, band_one, 1.0 - 2.0 * band_two]).real
    roots = np.array([(s + np.sqrt(s * s - 4.0)) / 2.0 for s in sums])
    roots = np.where(np.abs(roots) > 1.0, 1.0 / roots, roots)

    def right_side(z):
        return (
            rhs_one / 2.0 * (z - 1.0 / z)
            + rhs_two / 4.0 * (z**2 - z**-2)
            + rhs_three / 6.0 * (z**3 - z**-3)
        )

    weights = []
    for k in range(2):
        z, other = roots[k], roots[1 - k]
        slope = band_two * (z - 1.0 / z) * (z - other) * (z - 1.0 / other) / z
        weights.append(-right_side(z) / slope)
    direct = rhs_three / 6.0 / band_two
    offsets = np.arange(cells)[None, :] - np.arange(cells)[:, None]
    sizes = np.abs(offsets)
    matrix = sum(w * z**sizes for w, z in zip(weights, roots))
    matrix = np.sign(offsets) * (matrix + direct * (sizes == 1))
    edges = np.zeros((16, cells))
    place = np.arange(cells)
    low = np.zeros((cells, 8))
    high = np.zeros((cells, 8))
    for k in range(2):
        edges[k] = roots[k] ** (cells - 1 - place)
        edges[3 + k] = roots[k] ** place
        low[:, k] = -weights[k] * roots[k] ** (place + 1)
        high[:, 3 + k] = weights[k] * roots[k] ** (cells - place)
    edges[2, cells - 1] = 1.0
    edges[5, 0] = 1.0
    low[0, 2] = -direct
    high[cells - 1, 5] = direct
    full = np.concatenate([matrix, edges]).astype(np.float32)
    return full, edges[:8].astype(np.float32), low.astype(np.float32), high.astype(np.float32)


def halves_of(x):
    top = x.astype(bf16)
    return top, (x - top.astype(f32)).astype(bf16)


def dot_nn(a, b):
    return jnp.dot(a, b, preferred_element_type=f32)


def dot_nt(a, b):
    return lax.dot_general(a, b, (((1,), (1,)), ((), ())), preferred_element_type=f32)


def flux_kernel(
    rho_ref, vel_ref, thrust_ref, damp_ref, left_ref, right_ref, top_ref, rest_ref, low_ref, high_ref,
    rate_ref, edge_ref,
):
    cells = rho_ref.shape[0]
    u, v, w = vel_ref[0], vel_ref[1], vel_ref[2]
    u_top, u_rest = halves_of(u)
    top, rest = top_ref[:cells], rest_ref[:cells]
    dilatation = dot_nn(top, u_top) + dot_nn(rest, u_top) + dot_nn(top, u_rest)
    dilatation = dilatation + jnp.dot(low_ref[...], left_ref[...], precision=highest)
    dilatation = dilatation + jnp.dot(high_ref[...], right_ref[...], precision=highest)
    rho, thrust = rho_ref[...], thrust_ref[...]
    pressure = thrust - damp_ref[...] * dilatation
    energy = thrust / (gamma_gas - 1.0) + 0.5 * rho * (u * u + v * v + w * w)
    momentum = rho * u
    fluxes = [
        momentum,
        momentum * u + pressure,
        momentum * v,
        momentum * w,
        (energy + pressure) * u,
    ]
    for group in ((0, 1), (2, 3), (4,)):
        field = jnp.concatenate([fluxes[c] for c in group], axis=1)
        f_top, f_rest = halves_of(field)
        done = dot_nn(top_ref[...], f_top) + dot_nn(rest_ref[...], f_top) + dot_nn(top_ref[...], f_rest)
        for n, c in enumerate(group):
            rate_ref[c] = -done[:cells, n * 128 : (n + 1) * 128]
            edge_ref[c] = done[cells : cells + 8, n * 128 : (n + 1) * 128]


def bucket_of(cell):
    return (cell >> 15) * GROUPS + ((cell & 127) >> 5)


def fill_kernel(
    peer_ref, peers_ref, cell_ref, cells_ref, speed_ref, fluid_ref, thermal_ref, mass_ref,
    out_ref, top_ref, rest_ref, key_ref, hot_ref, count_ref, rank_ref, total_ref,
):
    peers = out_ref.shape[0] // 10
    blocks = peers_ref.shape[0]
    mass = mass_ref[...]
    work = adiabatic_exponent * mass * (thermal_ref[1:2, :] - thermal_ref[0:1, :])
    rows = []
    for c in range(3):
        speed = speed_ref[c : c + 1, :]
        force = mass * (fluid_ref[c : c + 1, :] - speed)
        work = work + force * speed
        rows.append(force)
    rows.append(work)
    rows.append((cell_ref[...] + 1).astype(f32))
    for c in range(5):
        top = rows[c].astype(bf16).astype(f32)
        top_ref[c : c + 1, :] = top
        rest_ref[c : c + 1, :] = rows[c] - top

    keys = (peers_ref[...] * BUCKETS + bucket_of(cells_ref[...])).astype(f32)
    key_ref[...] = keys
    turned = jnp.concatenate([keys, keys], axis=0).T
    peer_ids = lax.broadcasted_iota(jnp.int32, (peers, 128), 0).astype(bf16)
    bucket_ids = lax.broadcasted_iota(jnp.int32, (BUCKETS, 128), 0)
    earlier = lax.broadcasted_iota(jnp.int32, (128, 128), 0) < lax.broadcasted_iota(jnp.int32, (128, 128), 1)
    slot_ids = lax.broadcasted_iota(jnp.int32, (256, 128), 0).astype(bf16)
    zero = jnp.zeros((), bf16)
    one = jnp.ones((), bf16)

    def buckets_at(i):
        return bucket_of(cells_ref[pl.ds(i, 1), :]) == bucket_ids

    def count_step(t, carry):
        for k in range(CHUNK):
            i = t * CHUNK + k
            peer = peers_ref[pl.ds(i, 1), :].astype(f32).astype(bf16)
            hot = jnp.where(peer_ids == peer, one, zero)
            hot_ref[i] = hot
            mine = jnp.where(buckets_at(i), 1.0, 0.0).astype(bf16)
            count_ref[i] = dot_nt(mine, hot)
        return carry

    lax.fori_loop(0, blocks // CHUNK, count_step, 0)

    def base_step(i, before):
        now = count_ref[i]
        count_ref[i] = before
        return before + now

    counts = lax.fori_loop(0, blocks, base_step, jnp.zeros((BUCKETS, 128), f32))
    starts = [jnp.zeros((1, 128), f32)]
    for b in range(BUCKETS - 1):
        starts.append(starts[-1] + counts[b : b + 1, :])
    start = jnp.concatenate(starts, axis=0)

    def rank_step(t, rolled):
        for k in range(CHUNK):
            i = t * CHUNK + k
            same = (rolled[:, k : k + 1] == key_ref[pl.ds(i, 1), :]) & earlier
            inside = jnp.sum(jnp.where(same, 1.0, 0.0), axis=0, keepdims=True)
            base = dot_nn((count_ref[i] + start).astype(bf16), hot_ref[i])
            base = jnp.sum(jnp.where(buckets_at(i), base, 0.0), axis=0, keepdims=True)
            rank_ref[pl.ds(i, 1), :] = base + inside
        return pltpu.roll(rolled, 128 - CHUNK, 1)

    lax.fori_loop(0, blocks // CHUNK, rank_step, turned)

    total_ref[...] = jnp.zeros_like(total_ref)

    def place_step(t, carry):
        ranks, tops, rests = [], [], []
        for k in range(CHUNK):
            i = t * CHUNK + k
            here = pl.ds(pl.multiple_of(i * 128, 128), 128)
            rank = rank_ref[pl.ds(i, 1), :].astype(bf16)
            ranks.append(jnp.where(slot_ids == rank, one, zero))
            hot = hot_ref[i] != zero
            tops.append(
                jnp.concatenate(
                    [jnp.where(hot, top_ref[c : c + 1, here].astype(bf16), zero) for c in range(5)], axis=0
                )
            )
            rests.append(
                jnp.concatenate(
                    [jnp.where(hot, rest_ref[c : c + 1, here].astype(bf16), zero) for c in range(5)], axis=0
                )
            )
        ranks = jnp.concatenate(ranks, axis=1)
        total_ref[...] += dot_nt(jnp.concatenate(tops, axis=1), ranks) + dot_nt(
            jnp.concatenate(rests, axis=1), ranks
        )
        return carry

    lax.fori_loop(0, blocks // CHUNK, place_step, 0)
    for c in range(5):
        for h in range(2):
            out_ref[pl.ds(2 * c + h, peers, stride=10), :] = total_ref[
                c * peers : (c + 1) * peers, h * 128 : (h + 1) * 128
            ]


def bin_kernel(
    box_ref, rate_ref, left_ref, right_ref, low_ref, high_ref,
    out_ref, x_ref, l_ref, top_ref, rest_ref, total_ref,
):
    span = out_ref.shape[1] // HALVES
    lines = out_ref.shape[2] // GROUPS
    cells = []
    for h in range(2):
        here = slice(h * 128, (h + 1) * 128)
        for c in range(4):
            value = box_ref[pl.ds(2 * c + h, 128, stride=10), :].T
            top = value.astype(bf16).astype(f32)
            top_ref[c, here] = top
            rest_ref[c, here] = value - top
        cell = box_ref[pl.ds(8 + h, 128, stride=10), :].T.astype(jnp.int32) - 1
        x_ref[here] = (cell >> 7).astype(f32)
        l_ref[here] = (cell & 127).astype(f32)
        cells.append(cell)
    cell = jnp.concatenate(cells, axis=0)
    bucket = jnp.where(cell < 0, BUCKETS, bucket_of(cell))
    slot = lax.broadcasted_iota(jnp.int32, cell.shape, 0)
    total_ref[...] = jnp.zeros_like(total_ref)
    x_ids = lax.broadcasted_iota(jnp.int32, (span, 128), 0).astype(bf16)
    l_ids = lax.broadcasted_iota(jnp.int32, (lines, 128), 0).astype(bf16)
    zero = jnp.zeros((), bf16)
    one = jnp.ones((), bf16)
    for b in range(BUCKETS):
        half, group = b // GROUPS, b % GROUPS
        mine = bucket == b
        first = jnp.min(jnp.where(mine, slot, cell.shape[0]))
        last = jnp.max(jnp.where(mine, slot + STEP, 0))

        def step(t, carry, half=half, group=group, b=b):
            xs, tops, rests = [], [], []
            for k in range(STEP):
                row = pl.ds(t * STEP + k, 1)
                x = (x_ref[row, :] - float(half * span)).astype(bf16)
                xs.append(jnp.where(x_ids == x, one, zero))
                hot = l_ids == (l_ref[row, :] - float(group * lines)).astype(bf16)
                tops.append(
                    jnp.concatenate(
                        [jnp.where(hot, top_ref[c, row, :].astype(bf16), zero) for c in range(4)], axis=0
                    )
                )
                rests.append(
                    jnp.concatenate(
                        [jnp.where(hot, rest_ref[c, row, :].astype(bf16), zero) for c in range(4)], axis=0
                    )
                )
            xs = jnp.concatenate(xs, axis=1)
            total_ref[b] += dot_nt(jnp.concatenate(tops, axis=1), xs) + dot_nt(
                jnp.concatenate(rests, axis=1), xs
            )
            return carry

        lax.fori_loop(first // STEP, last // STEP, step, 0)
    for c in range(5):
        rate = rate_ref[c] - jnp.dot(low_ref[...], left_ref[c], precision=highest)
        rate = rate - jnp.dot(high_ref[...], right_ref[c], precision=highest)
        if c == 0:
            out_ref[c] = rate
            continue
        for half in range(HALVES):
            parts = [
                total_ref[half * GROUPS + g, (c - 1) * lines : c * lines, :] for g in range(GROUPS)
            ]
            deposit = jnp.concatenate(parts, axis=0).T
            here = slice(half * span, (half + 1) * span)
            out_ref[c, here] = rate[here] - deposit


def along(block, distance):
    count = lax.axis_size("line")
    return lax.ppermute(block, "line", [(i, (i + distance) % count) for i in range(count)])


def body(
    mass_per_volume,
    fluid_speed_field,
    fluid_thrust_field,
    shock_damping_field,
    grain_holding_processor,
    grain_mesh_slot,
    grain_speed_vector,
    fluid_speed_at_grain,
    thermal_states,
    grain_mass_over_lag,
):
    cells, lines = mass_per_volume.shape
    parts = grain_mesh_slot.shape[0]
    peers = lax.axis_size(("line", "slab"))
    full, edges, low, high = operator_tables(cells)
    full_top = full.astype(jnp.bfloat16)
    full_rest = (full - full_top.astype(np.float32)).astype(jnp.bfloat16)

    edge = jnp.dot(edges, fluid_speed_field[0], precision=highest)
    left, right = along(edge, 1), along(edge, -1)

    blocks = parts // 128
    outgoing = pl.pallas_call(
        fill_kernel,
        name="fill",
        out_shape=jax.ShapeDtypeStruct((peers * 10, 128), f32),
        scratch_shapes=[
            pltpu.VMEM((8, parts), f32),
            pltpu.VMEM((8, parts), f32),
            pltpu.VMEM((blocks, 128), f32),
            pltpu.VMEM((blocks, peers, 128), bf16),
            pltpu.VMEM((blocks, BUCKETS, peers), f32),
            pltpu.VMEM((blocks, 128), f32),
            pltpu.VMEM((5 * peers, 256), f32),
        ],
    )(
        grain_holding_processor.reshape(1, parts),
        grain_holding_processor.reshape(blocks, 128),
        grain_mesh_slot.reshape(1, parts),
        grain_mesh_slot.reshape(blocks, 128),
        grain_speed_vector,
        fluid_speed_at_grain,
        thermal_states,
        grain_mass_over_lag.reshape(1, parts),
    )
    arrived = lax.all_to_all(
        outgoing.reshape(peers, 5, 2, 128), ("line", "slab"), split_axis=0, concat_axis=0, tiled=True
    ).reshape(peers * 10, 128)

    rate, flux_edge = pl.pallas_call(
        flux_kernel,
        name="flux",
        out_shape=(
            jax.ShapeDtypeStruct((5, cells, lines), f32),
            jax.ShapeDtypeStruct((5, 8, lines), f32),
        ),
        cost_estimate=pl.CostEstimate(flops=4 * 10**9, bytes_accessed=4 * 10**6, transcendentals=0),
    )(
        mass_per_volume, fluid_speed_field, fluid_thrust_field, shock_damping_field,
        left, right, full_top, full_rest, low, high,
    )
    flux_left, flux_right = along(flux_edge, 1), along(flux_edge, -1)

    return pl.pallas_call(
        bin_kernel,
        name="bin",
        out_shape=jax.ShapeDtypeStruct((5, cells, lines), f32),
        scratch_shapes=[
            pltpu.VMEM((256, 128), f32),
            pltpu.VMEM((256, 128), f32),
            pltpu.VMEM((4, 256, 128), f32),
            pltpu.VMEM((4, 256, 128), f32),
            pltpu.VMEM((BUCKETS, 4 * lines // GROUPS, cells // HALVES), f32),
        ],
    )(arrived, rate, flux_left, flux_right, low, high)


def solution(mesh):
    placed = (
        P("line", "slab"),
        P(None, "line", "slab"),
        P("line", "slab"),
        P("line", "slab"),
        P(("line", "slab"), None),
        P(("line", "slab")),
        P(None, ("line", "slab")),
        P(None, ("line", "slab")),
        P(None, ("line", "slab")),
        P(("line", "slab")),
    )
    return jax.shard_map(
        body, mesh=mesh, in_specs=placed, out_specs=P(None, "line", "slab"), check_vma=False
    )
```

profile of v0, /device:TPU:31, one launch (start us, length us, event | category | flops | bytes accessed | tf_op | source)
XLA Modules:
  0.0 122.0 jit_solution(2889718673943419893)
XLA Ops:
  0.0 0.0 copy-start.3
  0.0 17.0 %fill.1 = f32[1280,128]{1,0:T(8,128)} custom-call(s32[1,8192]{1,0:T(1,128)} %bitcast.13, s32[64,128]{1,0:T(8,128)} %bitcast.14, s32[1,8192]{1,0:T(1,128)} %bitcast.15, s32[64,128]{1,0:T(8,128)} %bitcast.16, f32[3,8192]{1,0:T(4,128)} %speed_ref.1, f32[3,8192]{1,0:T(4,128)} %fluid_ref.1, f32[2,8192]{1,0:T(2,128)} %thermal_ref.1, f32[1,8192]{1,0:T(1,128)} %bitcast.17), custom_call_target="tpu_custom_call" | custom-call | tf_op jit(solution)/shard_map/fill/pallas_call | solution.py:318
  17.0 10.5 %all-to-all-start = ((f32[128,5,2,128]{3,2,1,0:T(2,128)}), f32[128,5,2,128]{3,2,1,0:T(2,128)S(1)}, u32[]{:S(2)}, u32[]{:S(2)}) async-start(f32[128,5,2,128]{3,2,1,0:T(2,128)} %bitcast.11), calls=%async_computation | async-start | bytes 1310720 | tf_op jit(solution)/shard_map/all_to_all | solution.py:341
  27.6 0.0 copy-done.3
  27.6 1.2 fusion
  28.8 0.4 collective-permute-start.1
  29.2 1.4 %collective-permute-start = (f32[8,128]{1,0:T(8,128)S(1)}, f32[8,128]{1,0:T(8,128)S(1)}, u32[]{:S(2)}, u32[]{:S(2)}) collective-permute-start(f32[8,128]{1,0:T(8,128)S(1)} %fusion), channel_id=1, source_target_pairs={{0,16},{16,32},{32,48},{48,64},{64,80},{80,96},{96,112},{112,0},{1... | collective-permute-start | bytes 12296 | tf_op jit(solution)/shard_map/ppermute | solution.py:292
  30.5 4.4 %collective-permute-done.1.right_ref = f32[8,128]{1,0:T(8,128)S(1)} collective-permute-done((f32[8,128]{1,0:T(8,128)S(1)}, f32[8,128]{1,0:T(8,128)S(1)}, u32[]{:S(2)}, u32[]{:S(2)}) %collective-permute-start.1) | collective-permute-done | bytes 4128 | tf_op jit(solution)/shard_map/ppermute | solution.py:292
  35.0 0.0 copy-start.4
  35.0 0.0 collective-permute-done.left_ref
  35.0 0.6 copy-done.4
  35.6 0.0 copy-start.5
  35.6 0.6 copy-done.5
  36.1 5.3 %flux.1 = (f32[5,512,128]{2,1,0:T(8,128)}, f32[5,8,128]{2,1,0:T(8,128)}) custom-call(f32[512,128]{1,0:T(8,128)} %rho_ref.1, f32[3,512,128]{2,1,0:T(8,128)} %vel_ref.1, f32[512,128]{1,0:T(8,128)} %thrust_ref.1, f32[512,128]{1,0:T(8,128)} %damp_ref.1, f32[8,128]{1,0:T(8,128)} %copy-done.5, f32[8,128]{1,0:T(8,128)} %copy-done.4, ...), custom_call_target="tpu_custom_call" | custom-call | flops 4000000000 | bytes 4000000 | tf_op jit(solution)/shard_map/flux/pallas_call | solution.py:345
  41.4 1.9 %collective-permute-start.3 = (f32[5,8,128]{2,1,0:T(8,128)}, f32[5,8,128]{2,1,0:T(8,128)S(1)}, u32[]{:S(2)}, u32[]{:S(2)}) collective-permute-start(f32[5,8,128]{2,1,0:T(8,128)} %get-tuple-element.8), channel_id=1, source_target_pairs={{0,112},{16,0},{32,16},{48,32},{64,48},{80,64},{96,80},{112,96},{1... | collective-permute-start | bytes 61448 | tf_op jit(solution)/shard_map/ppermute | solution.py:292
  43.3 0.0 collective-permute-start.2
  43.3 1.5 %collective-permute-done.3.right_ref = f32[5,8,128]{2,1,0:T(8,128)S(1)} collective-permute-done((f32[5,8,128]{2,1,0:T(8,128)}, f32[5,8,128]{2,1,0:T(8,128)S(1)}, u32[]{:S(2)}, u32[]{:S(2)}) %collective-permute-start.3) | collective-permute-done | bytes 20512 | tf_op jit(solution)/shard_map/ppermute | solution.py:292
  44.8 0.0 copy-start.1
  44.8 0.1 collective-permute-done.2.left_ref
  45.0 0.0 copy-start.2
  45.0 0.0 all-to-all-done
  45.0 0.0 copy-start
  45.0 0.5 copy-done.1
  45.4 0.1 copy-done.2
  45.5 0.2 copy-done
  45.8 76.2 %bin.1 = f32[5,512,128]{2,1,0:T(8,128)} custom-call(f32[1280,128]{1,0:T(8,128)} %bitcast.12, f32[5,512,128]{2,1,0:T(8,128)} %get-tuple-element.7.rate_ref, f32[5,8,128]{2,1,0:T(8,128)} %copy-done.2, f32[5,8,128]{2,1,0:T(8,128)} %copy-done.1, f32[512,8]{1,0:T(8,128)} %constant.13.clone.low_ref, f32[512,8]{1,0:T(8,128)} %constant.14.clone.high_ref), custom_call_target="tpu_custom_call" | custom-call | tf_op jit(solution)/shard_map/bin/pallas_call | solution.py:359
Async XLA Ops:
  0.0 27.6 %copy-start.3 = (f32[8,512]{1,0:T(8,128)S(1)}, f32[8,512]{1,0:T(8,128)}, u32[]{:S(2)}) copy-start(f32[8,512]{1,0:T(8,128)} %constant.10.clone) | copy-start | bytes 49156
  17.0 27.9 %all-to-all-start = ((f32[128,5,2,128]{3,2,1,0:T(2,128)}), f32[128,5,2,128]{3,2,1,0:T(2,128)S(1)}, u32[]{:S(2)}, u32[]{:S(2)}) async-start(f32[128,5,2,128]{3,2,1,0:T(2,128)} %bitcast.11), calls=%async_computation | async-start | bytes 1310720 | tf_op jit(solution)/shard_map/all_to_all | solution.py:341
  28.8 6.2 %collective-permute-start.1 = (f32[8,128]{1,0:T(8,128)S(1)}, f32[8,128]{1,0:T(8,128)S(1)}, u32[]{:S(2)}, u32[]{:S(2)}) collective-permute-start(f32[8,128]{1,0:T(8,128)S(1)} %fusion), channel_id=1, source_target_pairs={{0,112},{16,0},{32,16},{48,32},{64,48},{80,64},{96,80},{112,96},{1... | collective-permute-start | bytes 12296 | tf_op jit(solution)/shard_map/ppermute | solution.py:292
  29.2 5.8 %collective-permute-start = (f32[8,128]{1,0:T(8,128)S(1)}, f32[8,128]{1,0:T(8,128)S(1)}, u32[]{:S(2)}, u32[]{:S(2)}) collective-permute-start(f32[8,128]{1,0:T(8,128)S(1)} %fusion), channel_id=1, source_target_pairs={{0,16},{16,32},{32,48},{48,64},{64,80},{80,96},{96,112},{112,0},{1... | collective-permute-start | bytes 12296 | tf_op jit(solution)/shard_map/ppermute | solution.py:292
  35.0 0.6 copy-start.4
  35.6 0.6 copy-start.5
  41.4 3.4 %collective-permute-start.3 = (f32[5,8,128]{2,1,0:T(8,128)}, f32[5,8,128]{2,1,0:T(8,128)S(1)}, u32[]{:S(2)}, u32[]{:S(2)}) collective-permute-start(f32[5,8,128]{2,1,0:T(8,128)} %get-tuple-element.8), channel_id=1, source_target_pairs={{0,112},{16,0},{32,16},{48,32},{64,48},{80,64},{96,80},{112,96},{1... | collective-permute-start | bytes 61448 | tf_op jit(solution)/shard_map/ppermute | solution.py:292
  43.3 1.6 %collective-permute-start.2 = (f32[5,8,128]{2,1,0:T(8,128)}, f32[5,8,128]{2,1,0:T(8,128)S(1)}, u32[]{:S(2)}, u32[]{:S(2)}) collective-permute-start(f32[5,8,128]{2,1,0:T(8,128)} %get-tuple-element.8), channel_id=1, source_target_pairs={{0,16},{16,32},{32,48},{48,64},{64,80},{80,96},{96,112},{112,0},{1... | collective-permute-start | bytes 61448 | tf_op jit(solution)/shard_map/ppermute | solution.py:292
  44.8 0.6 copy-start.1
  45.0 0.6 copy-start.2
  45.0 0.8 copy-start
where the time goes:
time: 121 us; the launch traced here: 122 us
  Pallas kernels  98.5 us (81%)
  starting transfers between devices  14.2 us (12%)
  waiting for transfers between devices  6.09 us (5%)
  local copies, waits for them, and re-layouts  2.02 us (2%)
    pallas_call x1, Pallas kernels, body(): pl.pallas_call(bin_kernel, name='bin', out_shape=jax.ShapeDtypeStruct((5,...  76.2 us
    pallas_call x1, Pallas kernels, body(): pl.pallas_call(fill_kernel, name='fill', out_shape=jax.ShapeDtypeStruct((...  17 us
    all_to_all x1, starting transfers between devices, body(): lax.all_to_all(outgoing.reshape(peers, 5, 2, 128), ('line', 'slab'), spli...  10.5 us
    ppermute x4, waiting for transfers between devices, along(): lax.ppermute(block, 'line', [(i, (i + distance) % count) for i in range(c...  6.08 us
    pallas_call x1, Pallas kernels, body(): pl.pallas_call(flux_kernel, name='flux', out_shape=(jax.ShapeDtypeStruct(...  5.26 us
    ppermute x4, starting transfers between devices, along(): lax.ppermute(block, 'line', [(i, (i + distance) % count) for i in range(c...  3.66 us
  transfers between devices with their start and end apart: 5, of which 3 were waited for; matrix products, arithmetic and copies ran while one was open for 1% of the time, Pallas kernels for 4%

commit v1 on v0

v1 whole, which is shorter than its diff:
```python
import jax
import jax.numpy as jnp
import numpy as np
from jax import lax
from jax.experimental import pallas as pl
from jax.experimental.pallas import tpu as pltpu
from jax.sharding import PartitionSpec as P


band_one = 0.5
band_two = 0.05
rhs_one = 17.0 / 12.0
rhs_two = 101.0 / 150.0
rhs_three = 0.01
gamma_gas = 1.4
adiabatic_exponent = 0.6
highest = lax.Precision.HIGHEST
f32 = jnp.float32
bf16 = jnp.bfloat16

HALVES = 2
GROUPS = 4
BUCKETS = HALVES * GROUPS
STEP = 8
PAIR = 4
CHUNK = 16


def operator_tables(cells):
    sums = np.roots([band_two, band_one, 1.0 - 2.0 * band_two]).real
    roots = np.array([(s + np.sqrt(s * s - 4.0)) / 2.0 for s in sums])
    roots = np.where(np.abs(roots) > 1.0, 1.0 / roots, roots)

    def right_side(z):
        return (
            rhs_one / 2.0 * (z - 1.0 / z)
            + rhs_two / 4.0 * (z**2 - z**-2)
            + rhs_three / 6.0 * (z**3 - z**-3)
        )

    weights = []
    for k in range(2):
        z, other = roots[k], roots[1 - k]
        slope = band_two * (z - 1.0 / z) * (z - other) * (z - 1.0 / other) / z
        weights.append(-right_side(z) / slope)
    direct = rhs_three / 6.0 / band_two
    offsets = np.arange(cells)[None, :] - np.arange(cells)[:, None]
    sizes = np.abs(offsets)
    matrix = sum(w * z**sizes for w, z in zip(weights, roots))
    matrix = np.sign(offsets) * (matrix + direct * (sizes == 1))
    edges = np.zeros((16, cells))
    place = np.arange(cells)
    low = np.zeros((cells, 8))
    high = np.zeros((cells, 8))
    for k in range(2):
        edges[k] = roots[k] ** (cells - 1 - place)
        edges[3 + k] = roots[k] ** place
        low[:, k] = -weights[k] * roots[k] ** (place + 1)
        high[:, 3 + k] = weights[k] * roots[k] ** (cells - place)
    edges[2, cells - 1] = 1.0
    edges[5, 0] = 1.0
    low[0, 2] = -direct
    high[cells - 1, 5] = direct
    full = np.concatenate([matrix, edges]).astype(np.float32)
    return full, edges[:8].astype(np.float32), low.astype(np.float32), high.astype(np.float32)


def halves_of(x):
    top = x.astype(bf16)
    return top, (x - top.astype(f32)).astype(bf16)


def dot_nn(a, b):
    return jnp.dot(a, b, preferred_element_type=f32)


def dot_nt(a, b):
    return lax.dot_general(a, b, (((1,), (1,)), ((), ())), preferred_element_type=f32)


def flux_kernel(
    rho_ref, vel_ref, thrust_ref, damp_ref, left_ref, right_ref, full_ref, fix_ref,
    rate_ref, edge_ref,
):
    cells = rho_ref.shape[0]
    u, v, w = vel_ref[0], vel_ref[1], vel_ref[2]
    u_top, u_rest = halves_of(u)
    dilatation = dot_nn(full_ref[:cells], jnp.concatenate([u_top, u_top, u_rest], axis=0))
    sent_top, sent_rest = halves_of(jnp.concatenate([left_ref[...], right_ref[...]], axis=0))
    dilatation = dilatation + dot_nn(
        fix_ref[...], jnp.concatenate([sent_top, sent_top, sent_rest], axis=0)
    )
    rho, thrust = rho_ref[...], thrust_ref[...]
    pressure = thrust - damp_ref[...] * dilatation
    energy = thrust / (gamma_gas - 1.0) + 0.5 * rho * (u * u + v * v + w * w)
    momentum = rho * u
    fluxes = [
        momentum,
        momentum * u + pressure,
        momentum * v,
        momentum * w,
        (energy + pressure) * u,
    ]
    for group in ((0, 1), (2, 3), (4,)):
        field = jnp.concatenate([fluxes[c] for c in group], axis=1)
        f_top, f_rest = halves_of(field)
        done = dot_nn(full_ref[...], jnp.concatenate([f_top, f_top, f_rest], axis=0))
        for n, c in enumerate(group):
            rate_ref[c] = -done[:cells, n * 128 : (n + 1) * 128]
            edge_ref[c] = done[cells : cells + 8, n * 128 : (n + 1) * 128]


def spread(block, k, copies):
    wide = jnp.broadcast_to(block[k : k + 1, :], (16, 128)).astype(bf16)
    return jnp.concatenate([wide] * copies, axis=0)


def bucket_of(cell):
    return (cell >> 15) * GROUPS + ((cell & 127) >> 5)


def fill_kernel(
    peer_ref, peers_ref, cell_ref, cells_ref, speed_ref, fluid_ref, thermal_ref, mass_ref,
    out_ref, top_ref, rest_ref, key_ref, hot_ref, count_ref, total_ref,
):
    peers = out_ref.shape[0] // 10
    blocks = peers_ref.shape[0]
    mass = mass_ref[...]
    work = adiabatic_exponent * mass * (thermal_ref[1:2, :] - thermal_ref[0:1, :])
    rows = []
    for c in range(3):
        speed = speed_ref[c : c + 1, :]
        force = mass * (fluid_ref[c : c + 1, :] - speed)
        work = work + force * speed
        rows.append(force)
    rows.append(work)
    rows.append((cell_ref[...] + 1).astype(f32))
    for c in range(5):
        top = rows[c].astype(bf16).astype(f32)
        top_ref[c : c + 1, :] = top
        rest_ref[c : c + 1, :] = rows[c] - top

    keys = (peers_ref[...] * BUCKETS + bucket_of(cells_ref[...])).astype(f32)
    key_ref[...] = keys
    turned = jnp.concatenate([keys, keys], axis=0).T
    peer_ids = lax.broadcasted_iota(jnp.int32, (peers, 128), 0).astype(bf16)
    bucket_ids = lax.broadcasted_iota(jnp.int32, (BUCKETS, 128), 0)
    earlier = lax.broadcasted_iota(jnp.int32, (128, 128), 0) < lax.broadcasted_iota(jnp.int32, (128, 128), 1)
    slot_ids = lax.broadcasted_iota(jnp.int32, (256, 128), 0).astype(bf16)
    zero = jnp.zeros((), bf16)
    one = jnp.ones((), bf16)

    def buckets_at(block, k):
        return block[k : k + 1, :] == bucket_ids

    def count_step(t, carry):
        for n in range(2):
            rows = pl.ds(pl.multiple_of((2 * t + n) * CHUNK, CHUNK), CHUNK)
            peer_rows = peers_ref[rows, :].astype(f32)
            bucket_rows = bucket_of(cells_ref[rows, :])
            for k in range(CHUNK):
                i = (2 * t + n) * CHUNK + k
                hot = jnp.where(peer_ids == spread(peer_rows, k, peers // 16), one, zero)
                hot_ref[i] = hot
                mine = jnp.where(buckets_at(bucket_rows, k), 1.0, 0.0).astype(bf16)
                count_ref[i] = dot_nt(mine, hot)
        return carry

    lax.fori_loop(0, blocks // (2 * CHUNK), count_step, 0)

    def base_step(t, before):
        for k in range(CHUNK):
            now = count_ref[t * CHUNK + k]
            count_ref[t * CHUNK + k] = before
            before = before + now
        return before

    counts = lax.fori_loop(0, blocks // CHUNK, base_step, jnp.zeros((BUCKETS, 128), f32))
    room = [None] * BUCKETS
    left = jnp.full((1, 128), 256.0)
    for b in reversed(range(BUCKETS)):
        left = left - counts[b : b + 1, :]
        room[b] = left
    starts = []
    end = jnp.zeros((1, 128), f32)
    for b in range(BUCKETS):
        starts.append(jnp.minimum(jnp.maximum(end, float(b * 256 // BUCKETS)), room[b]))
        end = starts[-1] + counts[b : b + 1, :]
    start = jnp.concatenate(starts, axis=0)

    rounds = blocks // CHUNK

    def rank_rows(t, rolled):
        rows = pl.ds(pl.multiple_of(t * CHUNK, CHUNK), CHUNK)
        key_rows = key_ref[rows, :]
        bucket_rows = bucket_of(cells_ref[rows, :])
        ranks = []
        for k in range(CHUNK):
            i = t * CHUNK + k
            same = (rolled[:, k : k + 1] == key_rows[k : k + 1, :]) & earlier
            inside = jnp.sum(jnp.where(same, 1.0, 0.0), axis=0, keepdims=True)
            base = dot_nn((count_ref[i] + start).astype(bf16), hot_ref[i])
            base = jnp.sum(jnp.where(buckets_at(bucket_rows, k), base, 0.0), axis=0, keepdims=True)
            ranks.append(base + inside)
        return jnp.concatenate(ranks, axis=0), pltpu.roll(rolled, 128 - CHUNK, 1)

    total_ref[...] = jnp.zeros_like(total_ref)

    def place_step(t, carry):
        rank_rows_now, rolled = carry
        rows = pl.ds(pl.multiple_of(t * CHUNK, CHUNK), CHUNK)
        peer_rows = peers_ref[rows, :].astype(f32)
        sums = None
        for pair in range(CHUNK // PAIR):
            ranks, values = [], []
            for k in range(pair * PAIR, (pair + 1) * PAIR):
                here = pl.ds(pl.multiple_of((t * CHUNK + k) * 128, 128), 128)
                ranks.append(jnp.where(slot_ids == spread(rank_rows_now, k, 16), one, zero))
                hot = peer_ids == spread(peer_rows, k, peers // 16)
                top_rows, rest_rows = top_ref[:, here], rest_ref[:, here]
                parts = [jnp.where(hot, spread(top_rows, c, peers // 16), zero) for c in range(5)]
                parts += [jnp.where(hot, spread(rest_rows, c, peers // 16), zero) for c in range(5)]
                values.append(jnp.concatenate(parts, axis=0))
            ranks = jnp.concatenate(ranks, axis=1)
            part = dot_nt(jnp.concatenate(values, axis=1), ranks)
            sums = part if sums is None else sums + part
        following = rank_rows(jnp.minimum(t + 1, rounds - 1), rolled)
        total_ref[...] += sums
        return following

    lax.fori_loop(0, rounds, place_step, rank_rows(0, turned))
    for c in range(5):
        for h in range(2):
            here = slice(h * 128, (h + 1) * 128)
            out_ref[pl.ds(2 * c + h, peers, stride=10), :] = (
                total_ref[c * peers : (c + 1) * peers, here]
                + total_ref[(c + 5) * peers : (c + 6) * peers, here]
            )


def bin_kernel(
    box_ref, rate_ref, left_ref, right_ref, fix_ref,
    out_ref, x_ref, l_ref, value_ref, total_ref,
):
    span = out_ref.shape[1] // HALVES
    lines = out_ref.shape[2] // GROUPS
    slots = 256
    lows, highs = [], []
    for h in range(2):
        here = slice(h * 128, (h + 1) * 128)
        for c in range(4):
            value = box_ref[pl.ds(2 * c + h, 128, stride=10), :].T
            top = value.astype(bf16).astype(f32)
            value_ref[c, here] = top
            value_ref[4 + c, here] = value - top
        arrived = box_ref[pl.ds(8 + h, 128, stride=10), :]
        cell = arrived.T.astype(jnp.int32) - 1
        across = (cell >> 7).astype(f32)
        for half in range(HALVES):
            x_ref[half, here] = across - float(half * span)
        l_ref[here] = (cell & 127).astype(f32)
        cell = arrived.astype(jnp.int32) - 1
        bucket = jnp.where(cell < 0, BUCKETS, bucket_of(cell))
        slot = lax.broadcasted_iota(jnp.int32, (1, 128), 1).astype(f32) + float(h * 128)
        found = [
            jnp.max(jnp.where(bucket == b, 1.0, 0.0), axis=0, keepdims=True) for b in range(BUCKETS)
        ]
        found = jnp.concatenate(found, axis=0) > 0.0
        lows.append(jnp.where(found, slot, float(slots)))
        highs.append(jnp.where(found, slot + 1.0, 0.0))
    x_ref[:, slots:] = jnp.full((HALVES, x_ref.shape[1] - slots, 128), -512.0)
    l_ref[slots:] = jnp.zeros((l_ref.shape[0] - slots, 128), f32)
    value_ref[:, slots:] = jnp.zeros((8, value_ref.shape[1] - slots, 128), f32)
    low = jnp.min(jnp.minimum(lows[0], lows[1]), axis=1, keepdims=True)
    high = jnp.max(jnp.maximum(highs[0], highs[1]), axis=1, keepdims=True)
    low = (low.astype(jnp.int32) // STEP) * STEP
    rounds = (jnp.max(high.astype(jnp.int32) - low) + (STEP - 1)) // STEP
    firsts = [jnp.max(low[b : b + 1, :]) for b in range(BUCKETS)]
    total_ref[...] = jnp.zeros_like(total_ref)
    x_ids = lax.broadcasted_iota(jnp.int32, (span, 128), 0).astype(bf16)
    l_ids = [
        (lax.broadcasted_iota(jnp.int32, (lines, 128), 0) + g * lines).astype(bf16) for g in range(GROUPS)
    ]
    zero = jnp.zeros((), bf16)
    one = jnp.ones((), bf16)

    def step(t, carry):
        for b in range(BUCKETS):
            half, group = b // GROUPS, b % GROUPS
            first = pl.multiple_of(jnp.minimum(firsts[b] + t * STEP, slots), STEP)
            rows = pl.ds(first, STEP)
            x_rows, l_rows = x_ref[half, rows, :], l_ref[rows, :]
            value_rows = [value_ref[c, rows, :] for c in range(8)]
            sums = None
            for pair in range(STEP // PAIR):
                xs, values = [], []
                for k in range(pair * PAIR, (pair + 1) * PAIR):
                    xs.append(jnp.where(x_ids == spread(x_rows, k, span // 16), one, zero))
                    hot = l_ids[group] == spread(l_rows, k, lines // 16)
                    parts = [
                        jnp.where(hot, spread(value_rows[c], k, lines // 16), zero) for c in range(8)
                    ]
                    values.append(jnp.concatenate(parts, axis=0))
                xs = jnp.concatenate(xs, axis=1)
                part = dot_nt(jnp.concatenate(values, axis=1), xs)
                sums = part if sums is None else sums + part
            total_ref[b] += sums
        return carry

    lax.fori_loop(0, rounds, step, 0)
    sent = jnp.concatenate(
        [jnp.concatenate([left_ref[c], right_ref[c]], axis=0) for c in range(5)], axis=1
    )
    sent_top, sent_rest = halves_of(sent)
    shift = dot_nn(fix_ref[...], jnp.concatenate([sent_top, sent_top, sent_rest], axis=0))
    for c in range(5):
        rate = rate_ref[c] - shift[:, c * 128 : (c + 1) * 128]
        if c == 0:
            out_ref[c] = rate
            continue
        for half in range(HALVES):
            parts = [
                total_ref[half * GROUPS + g, (c - 1) * lines : c * lines, :]
                + total_ref[half * GROUPS + g, (c + 3) * lines : (c + 4) * lines, :]
                for g in range(GROUPS)
            ]
            deposit = jnp.concatenate(parts, axis=0).T
            here = slice(half * span, (half + 1) * span)
            out_ref[c, here] = rate[here] - deposit


def along(block, distance):
    count = lax.axis_size("line")
    return lax.ppermute(block, "line", [(i, (i + distance) % count) for i in range(count)])


def run_fill(
    peers, grain_holding_processor, grain_mesh_slot, grain_speed_vector, fluid_speed_at_grain,
    thermal_states, grain_mass_over_lag,
):
    parts = grain_mesh_slot.shape[0]
    blocks = parts // 128
    return pl.pallas_call(
        fill_kernel,
        name="fill",
        compiler_params=pltpu.CompilerParams(vmem_limit_bytes=20 << 20),
        out_shape=jax.ShapeDtypeStruct((peers * 10, 128), f32),
        scratch_shapes=[
            pltpu.VMEM((8, parts), f32),
            pltpu.VMEM((8, parts), f32),
            pltpu.VMEM((blocks, 128), f32),
            pltpu.VMEM((blocks, peers, 128), bf16),
            pltpu.VMEM((blocks, BUCKETS, peers), f32),
            pltpu.VMEM((10 * peers, 256), f32),
        ],
    )(
        grain_holding_processor.reshape(1, parts),
        grain_holding_processor.reshape(blocks, 128),
        grain_mesh_slot.reshape(1, parts),
        grain_mesh_slot.reshape(blocks, 128),
        grain_speed_vector,
        fluid_speed_at_grain,
        thermal_states,
        grain_mass_over_lag.reshape(1, parts),
    )


def run_bin(arrived, rate, flux_left, flux_right, fix):
    cells, lines = rate.shape[1:]
    return pl.pallas_call(
        bin_kernel,
        name="bin",
        compiler_params=pltpu.CompilerParams(vmem_limit_bytes=20 << 20),
        out_shape=jax.ShapeDtypeStruct((5, cells, lines), f32),
        scratch_shapes=[
            pltpu.VMEM((HALVES, 256 + 2 * STEP, 128), f32),
            pltpu.VMEM((256 + 2 * STEP, 128), f32),
            pltpu.VMEM((8, 256 + 2 * STEP, 128), f32),
            pltpu.VMEM((BUCKETS, 8 * lines // GROUPS, cells // HALVES), f32),
        ],
    )(arrived, rate, flux_left, flux_right, fix)


def body(
    mass_per_volume,
    fluid_speed_field,
    fluid_thrust_field,
    shock_damping_field,
    grain_holding_processor,
    grain_mesh_slot,
    grain_speed_vector,
    fluid_speed_at_grain,
    thermal_states,
    grain_mass_over_lag,
):
    cells, lines = mass_per_volume.shape
    peers = lax.axis_size(("line", "slab"))
    full, edges, low, high = operator_tables(cells)
    full_top = full.astype(jnp.bfloat16)
    full_rest = (full - full_top.astype(np.float32)).astype(jnp.bfloat16)
    full = np.concatenate([full_top, full_rest, full_top], axis=1)
    fix = np.concatenate([low, high], axis=1)
    fix_top = fix.astype(jnp.bfloat16)
    fix_rest = (fix - fix_top.astype(np.float32)).astype(jnp.bfloat16)
    fix = np.concatenate([fix_top, fix_rest, fix_top], axis=1)

    edge = jnp.dot(edges, fluid_speed_field[0], precision=highest)
    left = along(edge, 1)
    right = along(edge, -1)
    outgoing = run_fill(
        peers, grain_holding_processor, grain_mesh_slot, grain_speed_vector, fluid_speed_at_grain,
        thermal_states, grain_mass_over_lag,
    )
    arrived = lax.all_to_all(
        outgoing.reshape(peers, 5, 2, 128), ("line", "slab"), split_axis=0, concat_axis=0, tiled=True
    ).reshape(peers * 10, 128)

    rate, flux_edge = pl.pallas_call(
        flux_kernel,
        name="flux",
        compiler_params=pltpu.CompilerParams(vmem_limit_bytes=20 << 20),
        out_shape=(
            jax.ShapeDtypeStruct((5, cells, lines), f32),
            jax.ShapeDtypeStruct((5, 8, lines), f32),
        ),
        cost_estimate=pl.CostEstimate(flops=4 * 10**9, bytes_accessed=4 * 10**6, transcendentals=0),
    )(
        mass_per_volume, fluid_speed_field, fluid_thrust_field, shock_damping_field,
        left, right, full, fix,
    )
    flux_left, flux_right = along(flux_edge, 1), along(flux_edge, -1)

    return run_bin(arrived, rate, flux_left, flux_right, fix)


def solution(mesh):
    placed = (
        P("line", "slab"),
        P(None, "line", "slab"),
        P("line", "slab"),
        P("line", "slab"),
        P(("line", "slab"), None),
        P(("line", "slab")),
        P(None, ("line", "slab")),
        P(None, ("line", "slab")),
        P(None, ("line", "slab")),
        P(("line", "slab")),
    )
    return jax.shard_map(
        body, mesh=mesh, in_specs=placed, out_specs=P(None, "line", "slab"), check_vma=False
    )
```

time: 121 us -> 59.1 us (0.49)
  the two profiles are of different devices: /device:TPU:31 before, /device:TPU:4 now
where the time goes in v1:
time: 59.1 us; the launch traced here: 58.6 us
  Pallas kernels  27.4 us (46%)
  starting transfers between devices  14.1 us (24%)
  waiting for transfers between devices  9.42 us (16%)
  local copies, waits for them, and re-layouts  7.31 us (12%)
    pallas_call x1, Pallas kernels, run_bin(): pl.pallas_call(bin_kernel, name='bin', compiler_params=pltpu.CompilerPara...  15 us
    all_to_all x1, starting transfers between devices, body(): lax.all_to_all(outgoing.reshape(peers, 5, 2, 128), ('line', 'slab'), spli...  10.5 us
    pallas_call x1, Pallas kernels, run_fill(): pl.pallas_call(fill_kernel, name='fill', compiler_params=pltpu.CompilerPa...  9.94 us
    ppermute x4, waiting for transfers between devices, along(): lax.ppermute(block, 'line', [(i, (i + distance) % count) for i in range(c...  9.42 us
    unnamed x26, local copies, waits for them, and re-layouts  7.31 us
    ppermute x4, starting transfers between devices, along(): lax.ppermute(block, 'line', [(i, (i + distance) % count) for i in range(c...  3.62 us
    pallas_call x1, Pallas kernels, body(): pl.pallas_call(flux_kernel, name='flux', compiler_params=pltpu.CompilerPa...  2.53 us
  transfers between devices with their start and end apart: 5, of which 4 were waited for; matrix products, arithmetic and copies ran while one was open for 0% of the time, Pallas kernels for 4%

profile of v1, /device:TPU:4, one launch (start us, length us, event | category | flops | bytes accessed | tf_op | source)
XLA Modules:
  0.0 58.6 jit_solution(6128425669287890000)
XLA Ops:
  0.0 0.0 copy-start
  0.0 0.9 %copy-done = f32[3,8192]{1,0:T(4,128)S(1)} copy-done((f32[3,8192]{1,0:T(4,128)S(1)}, f32[3,8192]{1,0:T(4,128)}, u32[]{:S(2)}) %copy-start) | copy-done | bytes 98328
  0.9 0.0 copy-start.1
  0.9 0.9 %copy-done.1 = f32[3,8192]{1,0:T(4,128)S(1)} copy-done((f32[3,8192]{1,0:T(4,128)S(1)}, f32[3,8192]{1,0:T(4,128)}, u32[]{:S(2)}) %copy-start.1) | copy-done | bytes 98328
  1.8 0.0 copy-start.2
  1.8 0.8 %copy-done.2 = s32[8192,1]{0,1:T(1,128)S(1)} copy-done((s32[8192,1]{0,1:T(1,128)S(1)}, s32[8192,1]{0,1:T(1,128)}, u32[]{:S(2)}) %copy-start.2) | copy-done | bytes 32792
  2.6 0.0 copy-start.3
  2.6 0.8 %copy-done.3 = s32[8192]{0:T(1024)S(1)} copy-done((s32[8192]{0:T(1024)S(1)}, s32[8192]{0:T(1024)}, u32[]{:S(2)}) %copy-start.3) | copy-done | bytes 32792
  3.3 0.0 copy-start.6
  3.3 0.8 %copy-done.6 = f32[2,8192]{1,0:T(2,128)S(1)} copy-done((f32[2,8192]{1,0:T(2,128)S(1)}, f32[2,8192]{1,0:T(2,128)}, u32[]{:S(2)}) %copy-start.6) | copy-done | bytes 65560
  4.2 0.0 copy-start.7
  4.2 0.8 %copy-done.7 = f32[8192]{0:T(1024)S(1)} copy-done((f32[8192]{0:T(1024)S(1)}, f32[8192]{0:T(1024)}, u32[]{:S(2)}) %copy-start.7) | copy-done | bytes 32792
  4.9 0.0 copy-start.5
  4.9 0.0 copy-start.12
  4.9 0.0 copy-start.4
  4.9 0.0 copy-start.8
  4.9 0.0 copy-start.9
  4.9 9.9 %fill.1 = f32[1280,128]{1,0:T(8,128)} custom-call(s32[1,8192]{1,0:T(1,128)S(1)} %bitcast.12, s32[64,128]{1,0:T(8,128)S(1)} %bitcast.13, s32[1,8192]{1,0:T(1,128)S(1)} %bitcast.14, s32[64,128]{1,0:T(8,128)S(1)} %bitcast.15, f32[3,8192]{1,0:T(4,128)S(1)} %copy-done, f32[3,8192]{1,0:T(4,128)S(1)} %copy-done.1, f32[2,8192]{1,0:T(2,128)S(1)} %copy-done.6, ...), custom_call_target="tpu_custom_call" | custom-call | tf_op jit(solution)/shard_map/fill/pallas_call | solution.py:343
  14.9 10.5 %all-to-all-start = ((f32[128,5,2,128]{3,2,1,0:T(2,128)}), f32[128,5,2,128]{3,2,1,0:T(2,128)S(1)}, u32[]{:S(2)}, u32[]{:S(2)}) async-start(f32[128,5,2,128]{3,2,1,0:T(2,128)} %bitcast.5), calls=%async_computation | async-start | bytes 1310720 | tf_op jit(solution)/shard_map/all_to_all | solution.py:414
  25.4 0.0 copy-done.5
  25.4 0.0 copy-done.12
  25.4 0.2 fusion
  25.6 3.1 %collective-permute-start.1 = (f32[8,128]{1,0:T(8,128)S(1)}, f32[8,128]{1,0:T(8,128)S(1)}, u32[]{:S(2)}, u32[]{:S(2)}) collective-permute-start(f32[8,128]{1,0:T(8,128)S(1)} %fusion), channel_id=1, source_target_pairs={{0,112},{16,0},{32,16},{48,32},{64,48},{80,64},{96,80},{112,96},{1... | collective-permute-start | bytes 12296 | tf_op jit(solution)/shard_map/ppermute | solution.py:334
  28.8 0.0 collective-permute-start
  28.8 1.3 %collective-permute-done.1.right_ref = f32[8,128]{1,0:T(8,128)S(1)} collective-permute-done((f32[8,128]{1,0:T(8,128)S(1)}, f32[8,128]{1,0:T(8,128)S(1)}, u32[]{:S(2)}, u32[]{:S(2)}) %collective-permute-start.1) | collective-permute-done | bytes 4128 | tf_op jit(solution)/shard_map/ppermute | solution.py:334
  30.1 4.2 %collective-permute-done.left_ref = f32[8,128]{1,0:T(8,128)S(1)} collective-permute-done((f32[8,128]{1,0:T(8,128)S(1)}, f32[8,128]{1,0:T(8,128)S(1)}, u32[]{:S(2)}, u32[]{:S(2)}) %collective-permute-start) | collective-permute-done | bytes 4128 | tf_op jit(solution)/shard_map/ppermute | solution.py:334
  34.2 0.0 copy-done.4
  34.2 0.0 copy-done.8
  34.2 0.0 copy-done.9
  34.3 0.0 copy-start.10
  34.3 0.9 %copy-done.10 = f32[512,128]{1,0:T(8,128)S(1)} copy-done((f32[512,128]{1,0:T(8,128)S(1)}, f32[512,128]{1,0:T(8,128)}, u32[]{:S(2)}) %copy-start.10) | copy-done | bytes 262168
  35.2 0.0 copy-start.11
  35.2 1.4 %copy-done.11 = bf16[528,1536]{1,0:T(8,128)(2,1)S(1)} copy-done((bf16[528,1536]{1,0:T(8,128)(2,1)S(1)}, bf16[528,1536]{1,0:T(8,128)(2,1)}, u32[]{:S(2)}) %copy-start.11) | copy-done | bytes 1622040
  36.6 2.5 %flux.1 = (f32[5,512,128]{2,1,0:T(8,128)S(1)}, f32[5,8,128]{2,1,0:T(8,128)S(1)}) custom-call(f32[512,128]{1,0:T(8,128)S(1)} %copy-done.8, f32[3,512,128]{2,1,0:T(8,128)S(1)} %copy-done.5, f32[512,128]{1,0:T(8,128)S(1)} %copy-done.9, f32[512,128]{1,0:T(8,128)S(1)} %copy-done.10, f32[8,128]{1,0:T(8,128)S(1)} %collective-permute-done.left_ref, ...), custom_call_target="tpu_custom_call" | custom-call | flops 4000000000 | bytes 4000000 | tf_op jit(solution)/shard_map/flux/pallas_call | solution.py:418
  39.2 0.0 collective-permute-start.3
  39.2 0.5 collective-permute-start.2
  39.7 1.0 %collective-permute-done.3.right_ref = f32[5,8,128]{2,1,0:T(8,128)S(1)} collective-permute-done((f32[5,8,128]{2,1,0:T(8,128)S(1)}, f32[5,8,128]{2,1,0:T(8,128)S(1)}, u32[]{:S(2)}, u32[]{:S(2)}) %collective-permute-start.3) | collective-permute-done | bytes 20512 | tf_op jit(solution)/shard_map/ppermute | solution.py:334
  40.7 3.0 %collective-permute-done.2.left_ref = f32[5,8,128]{2,1,0:T(8,128)S(1)} collective-permute-done((f32[5,8,128]{2,1,0:T(8,128)S(1)}, f32[5,8,128]{2,1,0:T(8,128)S(1)}, u32[]{:S(2)}, u32[]{:S(2)}) %collective-permute-start.2) | collective-permute-done | bytes 20512 | tf_op jit(solution)/shard_map/ppermute | solution.py:334
  43.6 0.0 all-to-all-done
  43.6 15.0 %bin.1 = f32[5,512,128]{2,1,0:T(8,128)} custom-call(f32[1280,128]{1,0:T(8,128)S(1)} %bitcast.11, f32[5,512,128]{2,1,0:T(8,128)S(1)} %get-tuple-element.7.rate_ref, f32[5,8,128]{2,1,0:T(8,128)S(1)} %collective-permute-done.2.left_ref, f32[5,8,128]{2,1,0:T(8,128)S(1)} %collective-permute-done.3.right_ref, bf16[512,48]{1,0:T(8,128)(2,1)S(1)} %copy-done.4), custom_call_target="tpu_custom_call" | custom-call | tf_op jit(solution)/shard_map/bin/pallas_call | solution.py:370
Async XLA Ops:
  0.0 0.9 %copy-start = (f32[3,8192]{1,0:T(4,128)S(1)}, f32[3,8192]{1,0:T(4,128)}, u32[]{:S(2)}) copy-start(f32[3,8192]{1,0:T(4,128)} %speed_ref.1) | copy-start | bytes 294916
  0.9 0.9 %copy-start.1 = (f32[3,8192]{1,0:T(4,128)S(1)}, f32[3,8192]{1,0:T(4,128)}, u32[]{:S(2)}) copy-start(f32[3,8192]{1,0:T(4,128)} %fluid_ref.1) | copy-start | bytes 294916
  1.8 0.8 %copy-start.2 = (s32[8192,1]{0,1:T(1,128)S(1)}, s32[8192,1]{0,1:T(1,128)}, u32[]{:S(2)}) copy-start(s32[8192,1]{0,1:T(1,128)} %param.17) | copy-start | bytes 98308
  2.6 0.8 %copy-start.3 = (s32[8192]{0:T(1024)S(1)}, s32[8192]{0:T(1024)}, u32[]{:S(2)}) copy-start(s32[8192]{0:T(1024)} %param.18) | copy-start | bytes 98308
  3.3 0.8 %copy-start.6 = (f32[2,8192]{1,0:T(2,128)S(1)}, f32[2,8192]{1,0:T(2,128)}, u32[]{:S(2)}) copy-start(f32[2,8192]{1,0:T(2,128)} %thermal_ref.1) | copy-start | bytes 196612
  4.2 0.8 %copy-start.7 = (f32[8192]{0:T(1024)S(1)}, f32[8192]{0:T(1024)}, u32[]{:S(2)}) copy-start(f32[8192]{0:T(1024)} %param.22) | copy-start | bytes 98308
  4.9 20.5 %copy-start.5 = (f32[3,512,128]{2,1,0:T(8,128)S(1)}, f32[3,512,128]{2,1,0:T(8,128)}, u32[]{:S(2)}) copy-start(f32[3,512,128]{2,1,0:T(8,128)} %vel_ref.1) | copy-start | bytes 2359300
  4.9 20.5 %copy-start.12 = (f32[8,512]{1,0:T(8,128)S(1)}, f32[8,512]{1,0:T(8,128)}, u32[]{:S(2)}) copy-start(f32[8,512]{1,0:T(8,128)} %constant.6.clone) | copy-start | bytes 49156
  4.9 29.3 %copy-start.4 = (bf16[512,48]{1,0:T(8,128)(2,1)S(1)}, bf16[512,48]{1,0:T(8,128)(2,1)}, u32[]{:S(2)}) copy-start(bf16[512,48]{1,0:T(8,128)(2,1)} %constant.8.clone.fix_ref) | copy-start | bytes 147460
  4.9 29.3 %copy-start.8 = (f32[512,128]{1,0:T(8,128)S(1)}, f32[512,128]{1,0:T(8,128)}, u32[]{:S(2)}) copy-start(f32[512,128]{1,0:T(8,128)} %rho_ref.1) | copy-start | bytes 786436
  4.9 29.3 %copy-start.9 = (f32[512,128]{1,0:T(8,128)S(1)}, f32[512,128]{1,0:T(8,128)}, u32[]{:S(2)}) copy-start(f32[512,128]{1,0:T(8,128)} %thrust_ref.1) | copy-start | bytes 786436
  14.9 28.7 %all-to-all-start = ((f32[128,5,2,128]{3,2,1,0:T(2,128)}), f32[128,5,2,128]{3,2,1,0:T(2,128)S(1)}, u32[]{:S(2)}, u32[]{:S(2)}) async-start(f32[128,5,2,128]{3,2,1,0:T(2,128)} %bitcast.5), calls=%async_computation | async-start | bytes 1310720 | tf_op jit(solution)/shard_map/all_to_all | solution.py:414
  25.6 4.4 %collective-permute-start.1 = (f32[8,128]{1,0:T(8,128)S(1)}, f32[8,128]{1,0:T(8,128)S(1)}, u32[]{:S(2)}, u32[]{:S(2)}) collective-permute-start(f32[8,128]{1,0:T(8,128)S(1)} %fusion), channel_id=1, source_target_pairs={{0,112},{16,0},{32,16},{48,32},{64,48},{80,64},{96,80},{112,96},{1... | collective-permute-start | bytes 12296 | tf_op jit(solution)/shard_map/ppermute | solution.py:334
  28.8 5.5 %collective-permute-start = (f32[8,128]{1,0:T(8,128)S(1)}, f32[8,128]{1,0:T(8,128)S(1)}, u32[]{:S(2)}, u32[]{:S(2)}) collective-permute-start(f32[8,128]{1,0:T(8,128)S(1)} %fusion), channel_id=1, source_target_pairs={{0,16},{16,32},{32,48},{48,64},{64,80},{80,96},{96,112},{112,0},{1... | collective-permute-start | bytes 12296 | tf_op jit(solution)/shard_map/ppermute | solution.py:334
  34.3 1.0 %copy-start.10 = (f32[512,128]{1,0:T(8,128)S(1)}, f32[512,128]{1,0:T(8,128)}, u32[]{:S(2)}) copy-start(f32[512,128]{1,0:T(8,128)} %damp_ref.1) | copy-start | bytes 786436
  35.2 1.4 %copy-start.11 = (bf16[528,1536]{1,0:T(8,128)(2,1)S(1)}, bf16[528,1536]{1,0:T(8,128)(2,1)}, u32[]{:S(2)}) copy-start(bf16[528,1536]{1,0:T(8,128)(2,1)} %constant.7.clone.full_ref) | copy-start | bytes 4866052
  39.2 1.5 %collective-permute-start.3 = (f32[5,8,128]{2,1,0:T(8,128)S(1)}, f32[5,8,128]{2,1,0:T(8,128)S(1)}, u32[]{:S(2)}, u32[]{:S(2)}) collective-permute-start(f32[5,8,128]{2,1,0:T(8,128)S(1)} %get-tuple-element.8), channel_id=1, source_target_pairs={{0,112},{16,0},{32,16},{48,32},{64,48},{80,64},{96,80},{112,96},{1... | collective-permute-start | bytes 61448 | tf_op jit(solution)/shard_map/ppermute | solution.py:334
  39.2 4.4 %collective-permute-start.2 = (f32[5,8,128]{2,1,0:T(8,128)S(1)}, f32[5,8,128]{2,1,0:T(8,128)S(1)}, u32[]{:S(2)}, u32[]{:S(2)}) collective-permute-start(f32[5,8,128]{2,1,0:T(8,128)S(1)} %get-tuple-element.8), channel_id=1, source_target_pairs={{0,16},{16,32},{32,48},{48,64},{64,80},{80,96},{96,112},{112,0},{1... | collective-permute-start | bytes 61448 | tf_op jit(solution)/shard_map/ppermute | solution.py:334

commit v2 on v1

--- a/solution.py
+++ b/solution.py
@@ -1,3 +1,5 @@
+import functools
+
 import jax
 import jax.numpy as jnp
 import numpy as np
@@ -5,7 +7,6 @@
 from jax.experimental import pallas as pl
 from jax.experimental.pallas import tpu as pltpu
 from jax.sharding import PartitionSpec as P
-
 
 band_one = 0.5
 band_two = 0.05
@@ -26,6 +27,13 @@
 CHUNK = 16
 
 
+def stacked_of(table):
+    table = table.astype(np.float32)
+    top = table.astype(jnp.bfloat16)
+    rest = (table - top.astype(np.float32)).astype(jnp.bfloat16)
+    return np.concatenate([top, rest, top], axis=1)
+
+
 def operator_tables(cells):
     sums = np.roots([band_two, band_one, 1.0 - 2.0 * band_two]).real
     roots = np.array([(s + np.sqrt(s * s - 4.0)) / 2.0 for s in sums])
@@ -44,25 +52,37 @@
         slope = band_two * (z - 1.0 / z) * (z - other) * (z - 1.0 / other) / z
         weights.append(-right_side(z) / slope)
     direct = rhs_three / 6.0 / band_two
-    offsets = np.arange(cells)[None, :] - np.arange(cells)[:, None]
-    sizes = np.abs(offsets)
-    matrix = sum(w * z**sizes for w, z in zip(weights, roots))
-    matrix = np.sign(offsets) * (matrix + direct * (sizes == 1))
-    edges = np.zeros((16, cells))
     place = np.arange(cells)
-    low = np.zeros((cells, 8))
-    high = np.zeros((cells, 8))
+    reach = cells // 128
+    blocks = []
+    for apart in range(1 - reach, reach):
+        offsets = 128 * apart + place[None, :128] - place[:128, None]
+        sizes = np.abs(offsets)
+        block = sum(w * z**sizes for w, z in zip(weights, roots))
+        blocks.append(np.sign(offsets) * (block + direct * (sizes == 1)))
+    blocks = np.concatenate(blocks)
+    up, down = np.zeros((8, cells)), np.zeros((8, cells))
+    low, high = np.zeros((cells, 8)), np.zeros((cells, 8))
     for k in range(2):
-        edges[k] = roots[k] ** (cells - 1 - place)
-        edges[3 + k] = roots[k] ** place
+        up[k] = roots[k] ** (cells - 1 - place)
+        down[k] = roots[k] ** place
         low[:, k] = -weights[k] * roots[k] ** (place + 1)
-        high[:, 3 + k] = weights[k] * roots[k] ** (cells - place)
-    edges[2, cells - 1] = 1.0
-    edges[5, 0] = 1.0
+        high[:, k] = weights[k] * roots[k] ** (cells - place)
+    up[2, cells - 1] = 1.0
+    down[2, 0] = 1.0
     low[0, 2] = -direct
-    high[cells - 1, 5] = direct
-    full = np.concatenate([matrix, edges]).astype(np.float32)
-    return full, edges[:8].astype(np.float32), low.astype(np.float32), high.astype(np.float32)
+    high[cells - 1, 2] = direct
+    probe = []
+    for sums in (up, down):
+        mixed = np.zeros((24, cells))
+        for m in range(6):
+            added = low[:, m] if m < 3 else high[:, m - 3]
+            for k in range(3):
+                mixed[(m // 2) * 8 + (m % 2) * 4 + k] = sums[k] * added
+        probe += [sums, mixed]
+    probe = np.concatenate(probe)
+    fix = np.concatenate([low, high], axis=1)
+    return stacked_of(blocks)[:, :256], stacked_of(probe), stacked_of(fix)
 
 
 def halves_of(x):
@@ -78,36 +98,99 @@
     return lax.dot_general(a, b, (((1,), (1,)), ((), ())), preferred_element_type=f32)
 
 
-def flux_kernel(
-    rho_ref, vel_ref, thrust_ref, damp_ref, left_ref, right_ref, full_ref, fix_ref,
-    rate_ref, edge_ref,
-):
-    cells = rho_ref.shape[0]
+def stack_of(x):
+    top, rest = halves_of(x)
+    return jnp.concatenate([top, top, rest], axis=0)
+
+
+def operator_of(block_ref, cells):
+    reach = cells // 128
+    rows = []
+    for i in range(reach):
+        parts = []
+        for part in (0, 1, 0):
+            for j in range(reach):
+                n = j - i + reach - 1
+                parts.append(block_ref[n * 128 : (n + 1) * 128, part * 128 : (part + 1) * 128])
+        rows.append(jnp.concatenate(parts, axis=1))
+    return jnp.concatenate(rows, axis=0)
+
+
+def fluxes_of(rho, vel_ref, thrust, damp, dilatation):
     u, v, w = vel_ref[0], vel_ref[1], vel_ref[2]
-    u_top, u_rest = halves_of(u)
-    dilatation = dot_nn(full_ref[:cells], jnp.concatenate([u_top, u_top, u_rest], axis=0))
-    sent_top, sent_rest = halves_of(jnp.concatenate([left_ref[...], right_ref[...]], axis=0))
-    dilatation = dilatation + dot_nn(
-        fix_ref[...], jnp.concatenate([sent_top, sent_top, sent_rest], axis=0)
-    )
-    rho, thrust = rho_ref[...], thrust_ref[...]
-    pressure = thrust - damp_ref[...] * dilatation
+    pressure = thrust - damp * dilatation
     energy = thrust / (gamma_gas - 1.0) + 0.5 * rho * (u * u + v * v + w * w)
     momentum = rho * u
-    fluxes = [
+    return [
         momentum,
         momentum * u + pressure,
         momentum * v,
         momentum * w,
         (energy + pressure) * u,
     ]
+
+
+def edge_kernel(
+    rho_ref, vel_ref, thrust_ref, damp_ref, block_ref, probe_ref,
+    own_ref, up_ref, down_ref, far_up_ref, far_down_ref,
+):
+    cells, lines = rho_ref.shape
+    u, damp = vel_ref[0], damp_ref[...]
+    own = dot_nn(operator_of(block_ref, cells), stack_of(u))
+    own_ref[...] = own
+    fields = [u] + fluxes_of(rho_ref[...], vel_ref, thrust_ref[...], damp, own) + [damp, damp * u]
+    sums = dot_nn(probe_ref[...], stack_of(jnp.concatenate(fields, axis=1)))
+    for first, out_ref, far_ref in ((0, up_ref, far_up_ref), (32, down_ref, far_down_ref)):
+        for n in range(6):
+            out_ref[n * 8 : (n + 1) * 8] = sums[first : first + 8, n * lines : (n + 1) * lines]
+        for n in range(2):
+            here = slice((6 + n) * lines, (7 + n) * lines)
+            out_ref[48 + n * 24 : 72 + n * 24] = sums[first + 8 : first + 32, here]
+        far_ref[...] = sums[first : first + 8, :lines]
+
+
+def neighbour_sums(near_ref, low, high):
+    mix = [low[m : m + 1] for m in range(3)] + [high[m : m + 1] for m in range(3)]
+    wide = [jnp.broadcast_to(row, (4, row.shape[1])) for row in mix]
+    found = []
+    for c in range(5):
+        base = near_ref[(1 + c) * 8 : (2 + c) * 8]
+        if c in (1, 4):
+            first = 48 if c == 1 else 72
+            added = sum(
+                near_ref[first + q * 8 : first + (q + 1) * 8]
+                * jnp.concatenate([wide[2 * q], wide[2 * q + 1]], axis=0)
+                for q in range(3)
+            )
+            base = base - added - pltpu.roll(added, 4, 0)
+        found.append(base)
+    return jnp.concatenate(found, axis=1)
+
+
+def flux_kernel(
+    rho_ref, vel_ref, thrust_ref, damp_ref, own_ref, up_ref, down_ref,
+    left_ref, right_ref, far_left_ref, far_right_ref, block_ref, fix_ref, rate_ref,
+):
+    cells, lines = rho_ref.shape
+    full = operator_of(block_ref, cells)
+    near = jnp.concatenate([left_ref[:8], right_ref[:8]], axis=0)
+    dilatation = own_ref[...] + dot_nn(fix_ref[...], stack_of(near))
+    fluxes = fluxes_of(rho_ref[...], vel_ref, thrust_ref[...], damp_ref[...], dilatation)
+    sums = jnp.concatenate(
+        [
+            neighbour_sums(left_ref, far_left_ref[...], down_ref[:8]),
+            neighbour_sums(right_ref, up_ref[:8], far_right_ref[...]),
+        ],
+        axis=0,
+    )
+    added = dot_nn(fix_ref[...], stack_of(sums))
     for group in ((0, 1), (2, 3), (4,)):
         field = jnp.concatenate([fluxes[c] for c in group], axis=1)
-        f_top, f_rest = halves_of(field)
-        done = dot_nn(full_ref[...], jnp.concatenate([f_top, f_top, f_rest], axis=0))
+        done = dot_nn(full, stack_of(field))
         for n, c in enumerate(group):
-            rate_ref[c] = -done[:cells, n * 128 : (n + 1) * 128]
-            edge_ref[c] = done[cells : cells + 8, n * 128 : (n + 1) * 128]
+            rate_ref[c] = -(
+                done[:, n * lines : (n + 1) * lines] + added[:, c * lines : (c + 1) * lines]
+            )
 
 
 def spread(block, k, copies):
@@ -120,9 +203,19 @@
 
 
 def fill_kernel(
-    peer_ref, peers_ref, cell_ref, cells_ref, speed_ref, fluid_ref, thermal_ref, mass_ref,
-    out_ref, top_ref, rest_ref, key_ref, hot_ref, count_ref, total_ref,
+    *refs,
 ):
+    sources, out_ref, targets, sems = refs[:7], refs[7], refs[8:15], refs[15]
+    top_ref, rest_ref, key_ref, hot_ref, count_ref, total_ref = refs[16:]
+    peers_ref, cells_ref, cell_ref, speed_ref, fluid_ref, thermal_ref, mass_ref = targets
+    copies = [
+        pltpu.make_async_copy(source, target, sems.at[n])
+        for n, (source, target) in enumerate(zip(sources, targets))
+    ]
+    for copy in copies:
+        copy.start()
+    for copy in copies:
+        copy.wait()
     peers = out_ref.shape[0] // 10
     blocks = peers_ref.shape[0]
     mass = mass_ref[...]
@@ -239,8 +332,7 @@
 
 
 def bin_kernel(
-    box_ref, rate_ref, left_ref, right_ref, fix_ref,
-    out_ref, x_ref, l_ref, value_ref, total_ref,
+    box_ref, rate_ref, out_ref, x_ref, l_ref, value_ref, total_ref,
 ):
     span = out_ref.shape[1] // HALVES
     lines = out_ref.shape[2] // GROUPS
@@ -308,13 +400,8 @@
         return carry
 
     lax.fori_loop(0, rounds, step, 0)
-    sent = jnp.concatenate(
-        [jnp.concatenate([left_ref[c], right_ref[c]], axis=0) for c in range(5)], axis=1
-    )
-    sent_top, sent_rest = halves_of(sent)
-    shift = dot_nn(fix_ref[...], jnp.concatenate([sent_top, sent_top, sent_rest], axis=0))
     for c in range(5):
-        rate = rate_ref[c] - shift[:, c * 128 : (c + 1) * 128]
+        rate = rate_ref[c]
         if c == 0:
             out_ref[c] = rate
             continue
@@ -343,9 +430,19 @@
     return pl.pallas_call(
         fill_kernel,
         name="fill",
-        compiler_params=pltpu.CompilerParams(vmem_limit_bytes=20 << 20),
+        compiler_params=pltpu.CompilerParams(vmem_limit_bytes=60 << 20),
         out_shape=jax.ShapeDtypeStruct((peers * 10, 128), f32),
+        in_specs=[pl.BlockSpec(memory_space=pltpu.HBM)] * 7,
+        cost_estimate=pl.CostEstimate(flops=12 * 10**9, bytes_accessed=10**6, transcendentals=0),
         scratch_shapes=[
+            pltpu.VMEM((blocks, 128), jnp.int32),
+            pltpu.VMEM((blocks, 128), jnp.int32),
+            pltpu.VMEM((1, parts), jnp.int32),
+            pltpu.VMEM((3, parts), f32),
+            pltpu.VMEM((3, parts), f32),
+            pltpu.VMEM((2, parts), f32),
+            pltpu.VMEM((1, parts), f32),
+            pltpu.SemaphoreType.DMA((7,)),
             pltpu.VMEM((8, parts), f32),
             pltpu.VMEM((8, parts), f32),
             pltpu.VMEM((blocks, 128), f32),
@@ -354,10 +451,9 @@
             pltpu.VMEM((10 * peers, 256), f32),
         ],
     )(
-        grain_holding_processor.reshape(1, parts),
         grain_holding_processor.reshape(blocks, 128),
+        grain_mesh_slot.reshape(blocks, 128),
         grain_mesh_slot.reshape(1, parts),
-        grain_mesh_slot.reshape(blocks, 128),
         grain_speed_vector,
         fluid_speed_at_grain,
         thermal_states,
@@ -365,7 +461,7 @@
     )
 
 
-def run_bin(arrived, rate, flux_left, flux_right, fix):
+def run_bin(arrived, rate):
     cells, lines = rate.shape[1:]
     return pl.pallas_call(
         bin_kernel,
@@ -378,7 +474,7 @@
             pltpu.VMEM((8, 256 + 2 * STEP, 128), f32),
             pltpu.VMEM((BUCKETS, 8 * lines // GROUPS, cells // HALVES), f32),
         ],
-    )(arrived, rate, flux_left, flux_right, fix)
+    )(arrived, rate)
 
 
 def body(
@@ -395,18 +491,7 @@
 ):
     cells, lines = mass_per_volume.shape
     peers = lax.axis_size(("line", "slab"))
-    full, edges, low, high = operator_tables(cells)
-    full_top = full.astype(jnp.bfloat16)
-    full_rest = (full - full_top.astype(np.float32)).astype(jnp.bfloat16)
-    full = np.concatenate([full_top, full_rest, full_top], axis=1)
-    fix = np.concatenate([low, high], axis=1)
-    fix_top = fix.astype(jnp.bfloat16)
-    fix_rest = (fix - fix_top.astype(np.float32)).astype(jnp.bfloat16)
-    fix = np.concatenate([fix_top, fix_rest, fix_top], axis=1)
-
-    edge = jnp.dot(edges, fluid_speed_field[0], precision=highest)
-    left = along(edge, 1)
-    right = along(edge, -1)
+    blocks, probe, fix = operator_tables(cells)
     outgoing = run_fill(
         peers, grain_holding_processor, grain_mesh_slot, grain_speed_vector, fluid_speed_at_grain,
         thermal_states, grain_mass_over_lag,
@@ -415,22 +500,30 @@
         outgoing.reshape(peers, 5, 2, 128), ("line", "slab"), split_axis=0, concat_axis=0, tiled=True
     ).reshape(peers * 10, 128)
 
-    rate, flux_edge = pl.pallas_call(
+    gas = (mass_per_volume, fluid_speed_field, fluid_thrust_field, shock_damping_field)
+    own, up, down, far_up, far_down = pl.pallas_call(
+        edge_kernel,
+        name="edge",
+        compiler_params=pltpu.CompilerParams(vmem_limit_bytes=20 << 20),
+        out_shape=(
+            jax.ShapeDtypeStruct((cells, lines), f32),
+            jax.ShapeDtypeStruct((96, lines), f32),
+            jax.ShapeDtypeStruct((96, lines), f32),
+            jax.ShapeDtypeStruct((8, lines), f32),
+            jax.ShapeDtypeStruct((8, lines), f32),
+        ),
+        cost_estimate=pl.CostEstimate(flops=10**9, bytes_accessed=2 * 10**6, transcendentals=0),
+    )(*gas, blocks, probe)
+    left, right = along(up, 1), along(down, -1)
+    far_left, far_right = along(far_up, 2), along(far_down, -2)
+    rate = pl.pallas_call(
         flux_kernel,
         name="flux",
         compiler_params=pltpu.CompilerParams(vmem_limit_bytes=20 << 20),
-        out_shape=(
-            jax.ShapeDtypeStruct((5, cells, lines), f32),
-            jax.ShapeDtypeStruct((5, 8, lines), f32),
-        ),
-        cost_estimate=pl.CostEstimate(flops=4 * 10**9, bytes_accessed=4 * 10**6, transcendentals=0),
-    )(
-        mass_per_volume, fluid_speed_field, fluid_thrust_field, shock_damping_field,
-        left, right, full, fix,
-    )
-    flux_left, flux_right = along(flux_edge, 1), along(flux_edge, -1)
-
-    return run_bin(arrived, rate, flux_left, flux_right, fix)
+        out_shape=jax.ShapeDtypeStruct((5, cells, lines), f32),
+        cost_estimate=pl.CostEstimate(flops=2 * 10**9, bytes_accessed=4 * 10**6, transcendentals=0),
+    )(*gas, own, up, down, left, right, far_left, far_right, blocks, fix)
+    return run_bin(arrived, rate)
 
 
 def solution(mesh):
@@ -446,6 +539,7 @@
         P(None, ("line", "slab")),
         P(("line", "slab")),
     )
-    return jax.shard_map(
+    step = jax.shard_map(
         body, mesh=mesh, in_specs=placed, out_specs=P(None, "line", "slab"), check_vma=False
     )
+    return step

time: 59.1 us -> 50.8 us (0.86)
  the two profiles are of different devices: /device:TPU:4 before, /device:TPU:11 now
where the time goes in v2:
time: 50.8 us; the launch traced here: 51.3 us
  Pallas kernels  30.7 us (60%)
  starting transfers between devices  15.1 us (30%)
  waiting for transfers between devices  5.36 us (11%)
    pallas_call x1, Pallas kernels, run_bin(): pl.pallas_call(bin_kernel, name='bin', compiler_params=pltpu.CompilerPara...  16.2 us
    pallas_call x1, Pallas kernels, run_fill(): pl.pallas_call(fill_kernel, name='fill', compiler_params=pltpu.CompilerPa...  11.1 us
    all_to_all x1, starting transfers between devices, body(): lax.all_to_all(outgoing.reshape(peers, 5, 2, 128), ('line', 'slab'), spli...  10.7 us
    ppermute x4, waiting for transfers between devices, along(): lax.ppermute(block, 'line', [(i, (i + distance) % count) for i in range(c...  4.48 us
    ppermute x4, starting transfers between devices, along(): lax.ppermute(block, 'line', [(i, (i + distance) % count) for i in range(c...  4.35 us
    pallas_call x1, Pallas kernels, body(): pl.pallas_call(flux_kernel, name='flux', compiler_params=pltpu.CompilerPa...  1.71 us
    pallas_call x1, Pallas kernels, body(): pl.pallas_call(edge_kernel, name='edge', compiler_params=pltpu.CompilerPa...  1.7 us
  transfers between devices with their start and end apart: 5, of which 2 were waited for; matrix products, arithmetic and copies ran while one was open for 0% of the time, Pallas kernels for 7%

profile of v2, /device:TPU:11, one launch (start us, length us, event | category | flops | bytes accessed | tf_op | source)
XLA Modules:
  0.0 51.3 jit_solution(2445657713346953930)
XLA Ops:
  0.0 0.0 copy-start.3
  0.0 0.0 copy-start.4
  0.0 0.0 copy-start.6
  0.0 11.1 %fill.1 = f32[1280,128]{1,0:T(8,128)} custom-call(s32[64,128]{1,0:T(8,128)} %bitcast.8, s32[64,128]{1,0:T(8,128)} %bitcast.9, s32[1,8192]{1,0:T(1,128)} %bitcast.10, f32[3,8192]{1,0:T(4,128)} %refs_3_.1, f32[3,8192]{1,0:T(4,128)} %refs_4_.1, f32[2,8192]{1,0:T(2,128)} %refs_5_.1, f32[1,8192]{1,0:T(1,128)} %bitcast.11), custom_call_target="tpu_custom_call" | custom-call | flops 12000000000 | bytes 1000000 | tf_op jit(solution)/shard_map/fill/pallas_call | solution.py:430
  11.1 0.0 copy-start
  11.1 0.0 copy-start.1
  11.1 0.0 copy-start.2
  11.2 10.7 %all-to-all-start = ((f32[128,5,2,128]{3,2,1,0:T(2,128)}), f32[128,5,2,128]{3,2,1,0:T(2,128)S(1)}, u32[]{:S(2)}, u32[]{:S(2)}) async-start(f32[128,5,2,128]{3,2,1,0:T(2,128)} %bitcast.7), calls=%async_computation | async-start | bytes 1310720 | tf_op jit(solution)/shard_map/all_to_all | solution.py:499
  21.9 0.0 copy-done.3
  21.9 0.0 copy-done.4
  21.9 0.0 copy-done.6
  21.9 0.0 copy-done
  21.9 0.0 copy-done.1
  21.9 0.0 copy-done.2
  21.9 0.0 copy-start.5
  21.9 0.0 copy-start.7
  22.0 1.7 %edge.1 = (f32[512,128]{1,0:T(8,128)S(1)}, f32[96,128]{1,0:T(8,128)S(1)}, f32[96,128]{1,0:T(8,128)S(1)}, f32[8,128]{1,0:T(8,128)S(1)}, f32[8,128]{1,0:T(8,128)S(1)}) custom-call(f32[512,128]{1,0:T(8,128)S(1)} %copy-done.1, f32[3,512,128]{2,1,0:T(8,128)S(1)} %copy-done, f32[512,128]{1,0:T(8,128)S(1)} %copy-done.2, f32[512,128]{1,0:T(8,128)S(1)} %copy-done.3, ...), custom_call_target="tpu_custom_call" | custom-call | flops 1000000000 | bytes 2000000 | tf_op jit(solution)/shard_map/edge/pallas_call | solution.py:504
  23.7 1.7 %collective-permute-start = (f32[96,128]{1,0:T(8,128)S(1)}, f32[96,128]{1,0:T(8,128)S(1)}, u32[]{:S(2)}, u32[]{:S(2)}) collective-permute-start(f32[96,128]{1,0:T(8,128)S(1)} %get-tuple-element.11.up_ref), channel_id=1, source_target_pairs={{0,16},{16,32},{32,48},{48,64},{64,80},{80,96},{96,112},{112,0},{1... | collective-permute-start | bytes 147464 | tf_op jit(solution)/shard_map/ppermute | solution.py:421
  25.3 0.0 collective-permute-start.1
  25.3 1.4 %collective-permute-start.2 = (f32[8,128]{1,0:T(8,128)S(1)}, f32[8,128]{1,0:T(8,128)S(1)}, u32[]{:S(2)}, u32[]{:S(2)}) collective-permute-start(f32[8,128]{1,0:T(8,128)S(1)} %get-tuple-element.13), channel_id=1, source_target_pairs={{0,32},{16,48},{32,64},{48,80},{64,96},{80,112},{96,0},{112,16},{1... | collective-permute-start | bytes 12296 | tf_op jit(solution)/shard_map/ppermute | solution.py:421
  26.8 1.2 %collective-permute-start.3 = (f32[8,128]{1,0:T(8,128)S(1)}, f32[8,128]{1,0:T(8,128)S(1)}, u32[]{:S(2)}, u32[]{:S(2)}) collective-permute-start(f32[8,128]{1,0:T(8,128)S(1)} %get-tuple-element.14), channel_id=1, source_target_pairs={{0,96},{16,112},{32,0},{48,16},{64,32},{80,48},{96,64},{112,80},{1... | collective-permute-start | bytes 12296 | tf_op jit(solution)/shard_map/ppermute | solution.py:421
  28.0 4.5 %collective-permute-done.2.far_left_ref = f32[8,128]{1,0:T(8,128)S(1)} collective-permute-done((f32[8,128]{1,0:T(8,128)S(1)}, f32[8,128]{1,0:T(8,128)S(1)}, u32[]{:S(2)}, u32[]{:S(2)}) %collective-permute-start.2) | collective-permute-done | bytes 4128 | tf_op jit(solution)/shard_map/ppermute | solution.py:421
  32.5 0.0 collective-permute-done.3.far_right_ref
  32.5 0.0 collective-permute-done.left_ref
  32.5 0.0 collective-permute-done.1.right_ref
  32.5 0.0 copy-done.5
  32.5 0.0 copy-done.7
  32.5 1.7 %flux.1.rate_ref = f32[5,512,128]{2,1,0:T(8,128)S(1)} custom-call(f32[512,128]{1,0:T(8,128)S(1)} %copy-done.1, f32[3,512,128]{2,1,0:T(8,128)S(1)} %copy-done, f32[512,128]{1,0:T(8,128)S(1)} %copy-done.2, f32[512,128]{1,0:T(8,128)S(1)} %copy-done.3, f32[512,128]{1,0:T(8,128)S(1)} %get-tuple-element.10.own_ref, f32[96,128]{1,0:T(8,128)S(1)} %get-tuple-element.11.up_ref, ...), custom_call_target="tpu_custom_call" | custom-call | flops 2000000000 | bytes 4000000 | tf_op jit(solution)/shard_map/flux/pallas_call | solution.py:519
  34.2 0.9 %all-to-all-done = f32[128,5,2,128]{3,2,1,0:T(2,128)S(1)} async-done(((f32[128,5,2,128]{3,2,1,0:T(2,128)}), f32[128,5,2,128]{3,2,1,0:T(2,128)S(1)}, u32[]{:S(2)}, u32[]{:S(2)}) %all-to-all-start) | async-done | bytes 655392 | tf_op jit(solution)/shard_map/all_to_all | solution.py:499
  35.1 16.2 %bin.1 = f32[5,512,128]{2,1,0:T(8,128)} custom-call(f32[1280,128]{1,0:T(8,128)S(1)} %bitcast.6, f32[5,512,128]{2,1,0:T(8,128)S(1)} %flux.1.rate_ref), custom_call_target="tpu_custom_call" | custom-call | tf_op jit(solution)/shard_map/bin/pallas_call | solution.py:466
Async XLA Ops:
  0.0 21.9 %copy-start.3 = (f32[512,128]{1,0:T(8,128)S(1)}, f32[512,128]{1,0:T(8,128)}, u32[]{:S(2)}) copy-start(f32[512,128]{1,0:T(8,128)} %damp_ref.3) | copy-start | bytes 786436
  0.0 21.9 %copy-start.4 = (bf16[896,256]{1,0:T(8,128)(2,1)S(1)}, bf16[896,256]{1,0:T(8,128)(2,1)}, u32[]{:S(2)}) copy-start(bf16[896,256]{1,0:T(8,128)(2,1)} %constant.6.clone.block_ref) | copy-start | bytes 1376260
  0.0 21.9 %copy-start.6 = (bf16[64,1536]{1,0:T(8,128)(2,1)S(1)}, bf16[64,1536]{1,0:T(8,128)(2,1)}, u32[]{:S(2)}) copy-start(bf16[64,1536]{1,0:T(8,128)(2,1)} %constant.7.clone.probe_ref) | copy-start | bytes 589828
  11.1 10.8 %copy-start = (f32[3,512,128]{2,1,0:T(8,128)S(1)}, f32[3,512,128]{2,1,0:T(8,128)}, u32[]{:S(2)}) copy-start(f32[3,512,128]{2,1,0:T(8,128)} %vel_ref.3) | copy-start | bytes 2359300
  11.1 10.8 %copy-start.1 = (f32[512,128]{1,0:T(8,128)S(1)}, f32[512,128]{1,0:T(8,128)}, u32[]{:S(2)}) copy-start(f32[512,128]{1,0:T(8,128)} %rho_ref.3) | copy-start | bytes 786436
  11.1 10.8 %copy-start.2 = (f32[512,128]{1,0:T(8,128)S(1)}, f32[512,128]{1,0:T(8,128)}, u32[]{:S(2)}) copy-start(f32[512,128]{1,0:T(8,128)} %thrust_ref.3) | copy-start | bytes 786436
  11.2 24.0 %all-to-all-start = ((f32[128,5,2,128]{3,2,1,0:T(2,128)}), f32[128,5,2,128]{3,2,1,0:T(2,128)S(1)}, u32[]{:S(2)}, u32[]{:S(2)}) async-start(f32[128,5,2,128]{3,2,1,0:T(2,128)} %bitcast.7), calls=%async_computation | async-start | bytes 1310720 | tf_op jit(solution)/shard_map/all_to_all | solution.py:499
  21.9 10.6 %copy-start.5 = (bf16[896,256]{1,0:T(8,128)(2,1)S(1)}, bf16[896,256]{1,0:T(8,128)(2,1)}, u32[]{:S(2)}) copy-start(bf16[896,256]{1,0:T(8,128)(2,1)} %constant.6.clone.block_ref) | copy-start | bytes 1376260
  21.9 10.6 %copy-start.7 = (bf16[512,48]{1,0:T(8,128)(2,1)S(1)}, bf16[512,48]{1,0:T(8,128)(2,1)}, u32[]{:S(2)}) copy-start(bf16[512,48]{1,0:T(8,128)(2,1)} %constant.8.clone.fix_ref) | copy-start | bytes 147460
  23.7 8.8 %collective-permute-start = (f32[96,128]{1,0:T(8,128)S(1)}, f32[96,128]{1,0:T(8,128)S(1)}, u32[]{:S(2)}, u32[]{:S(2)}) collective-permute-start(f32[96,128]{1,0:T(8,128)S(1)} %get-tuple-element.11.up_ref), channel_id=1, source_target_pairs={{0,16},{16,32},{32,48},{48,64},{64,80},{80,96},{96,112},{112,0},{1... | collective-permute-start | bytes 147464 | tf_op jit(solution)/shard_map/ppermute | solution.py:421
  25.3 7.2 %collective-permute-start.1 = (f32[96,128]{1,0:T(8,128)S(1)}, f32[96,128]{1,0:T(8,128)S(1)}, u32[]{:S(2)}, u32[]{:S(2)}) collective-permute-start(f32[96,128]{1,0:T(8,128)S(1)} %get-tuple-element.12.down_ref), channel_id=1, source_target_pairs={{0,112},{16,0},{32,16},{48,32},{64,48},{80,64},{96,80},{112,96},{1... | collective-permute-start | bytes 147464 | tf_op jit(solution)/shard_map/ppermute | solution.py:421
  25.3 7.1 %collective-permute-start.2 = (f32[8,128]{1,0:T(8,128)S(1)}, f32[8,128]{1,0:T(8,128)S(1)}, u32[]{:S(2)}, u32[]{:S(2)}) collective-permute-start(f32[8,128]{1,0:T(8,128)S(1)} %get-tuple-element.13), channel_id=1, source_target_pairs={{0,32},{16,48},{32,64},{48,80},{64,96},{80,112},{96,0},{112,16},{1... | collective-permute-start | bytes 12296 | tf_op jit(solution)/shard_map/ppermute | solution.py:421
  26.8 5.7 %collective-permute-start.3 = (f32[8,128]{1,0:T(8,128)S(1)}, f32[8,128]{1,0:T(8,128)S(1)}, u32[]{:S(2)}, u32[]{:S(2)}) collective-permute-start(f32[8,128]{1,0:T(8,128)S(1)} %get-tuple-element.14), channel_id=1, source_target_pairs={{0,96},{16,112},{32,0},{48,16},{64,32},{80,48},{96,64},{112,80},{1... | collective-permute-start | bytes 12296 | tf_op jit(solution)/shard_map/ppermute | solution.py:421

commit v3 on v2

--- a/solution.py
+++ b/solution.py
@@ -24,7 +24,9 @@
 BUCKETS = HALVES * GROUPS
 STEP = 8
 PAIR = 4
+RING_SHIFT = 4
 CHUNK = 16
+FILL_PAIR = 4
 
 
 def stacked_of(table):
@@ -198,6 +200,11 @@
     return jnp.concatenate([wide] * copies, axis=0)
 
 
+def wrapped(slot):
+    slot = jnp.where(slot >= 256.0, slot - 256.0, slot)
+    return jnp.where(slot < 0.0, slot + 256.0, slot)
+
+
 def bucket_of(cell):
     return (cell >> 15) * GROUPS + ((cell & 127) >> 5)
 
@@ -279,7 +286,11 @@
     for b in range(BUCKETS):
         starts.append(jnp.minimum(jnp.maximum(end, float(b * 256 // BUCKETS)), room[b]))
         end = starts[-1] + counts[b : b + 1, :]
-    start = jnp.concatenate(starts, axis=0)
+    drifts = [starts[b] - float(b * 256 // BUCKETS) for b in range(BUCKETS)]
+    turn = float(RING_SHIFT) - jnp.floor(
+        (functools.reduce(jnp.maximum, drifts) + functools.reduce(jnp.minimum, drifts)) * 0.5
+    )
+    start = jnp.concatenate([wrapped(x + turn) for x in starts], axis=0)
 
     rounds = blocks // CHUNK
 
@@ -292,9 +303,9 @@
             i = t * CHUNK + k
             same = (rolled[:, k : k + 1] == key_rows[k : k + 1, :]) & earlier
             inside = jnp.sum(jnp.where(same, 1.0, 0.0), axis=0, keepdims=True)
-            base = dot_nn((count_ref[i] + start).astype(bf16), hot_ref[i])
+            base = dot_nn(wrapped(count_ref[i] + start).astype(bf16), hot_ref[i])
             base = jnp.sum(jnp.where(buckets_at(bucket_rows, k), base, 0.0), axis=0, keepdims=True)
-            ranks.append(base + inside)
+            ranks.append(wrapped(base + inside))
         return jnp.concatenate(ranks, axis=0), pltpu.roll(rolled, 128 - CHUNK, 1)
 
     total_ref[...] = jnp.zeros_like(total_ref)
@@ -304,9 +315,9 @@
         rows = pl.ds(pl.multiple_of(t * CHUNK, CHUNK), CHUNK)
         peer_rows = peers_ref[rows, :].astype(f32)
         sums = None
-        for pair in range(CHUNK // PAIR):
+        for pair in range(CHUNK // FILL_PAIR):
             ranks, values = [], []
-            for k in range(pair * PAIR, (pair + 1) * PAIR):
+            for k in range(pair * FILL_PAIR, (pair + 1) * FILL_PAIR):
                 here = pl.ds(pl.multiple_of((t * CHUNK + k) * 128, 128), 128)
                 ranks.append(jnp.where(slot_ids == spread(rank_rows_now, k, 16), one, zero))
                 hot = peer_ids == spread(peer_rows, k, peers // 16)
@@ -332,8 +343,10 @@
 
 
 def bin_kernel(
-    box_ref, rate_ref, out_ref, x_ref, l_ref, value_ref, total_ref,
+    box_ref, rate_ref, out_ref, x_ref, l_ref, value_ref, total_ref, done_ref, sems,
 ):
+    mass_copy = pltpu.make_async_copy(rate_ref.at[0], out_ref.at[0], sems.at[0])
+    mass_copy.start()
     span = out_ref.shape[1] // HALVES
     lines = out_ref.shape[2] // GROUPS
     slots = 256
@@ -353,21 +366,27 @@
         l_ref[here] = (cell & 127).astype(f32)
         cell = arrived.astype(jnp.int32) - 1
         bucket = jnp.where(cell < 0, BUCKETS, bucket_of(cell))
-        slot = lax.broadcasted_iota(jnp.int32, (1, 128), 1).astype(f32) + float(h * 128)
+        slot = lax.broadcasted_iota(jnp.int32, (BUCKETS, 128), 1) + h * 128
+        share = lax.broadcasted_iota(jnp.int32, (BUCKETS, 128), 0) * (slots // BUCKETS)
+        slot = (((slot - share + slots // 2) & (slots - 1)) - slots // 2).astype(f32)
         found = [
             jnp.max(jnp.where(bucket == b, 1.0, 0.0), axis=0, keepdims=True) for b in range(BUCKETS)
         ]
         found = jnp.concatenate(found, axis=0) > 0.0
         lows.append(jnp.where(found, slot, float(slots)))
-        highs.append(jnp.where(found, slot + 1.0, 0.0))
-    x_ref[:, slots:] = jnp.full((HALVES, x_ref.shape[1] - slots, 128), -512.0)
-    l_ref[slots:] = jnp.zeros((l_ref.shape[0] - slots, 128), f32)
-    value_ref[:, slots:] = jnp.zeros((8, value_ref.shape[1] - slots, 128), f32)
-    low = jnp.min(jnp.minimum(lows[0], lows[1]), axis=1, keepdims=True)
+        highs.append(jnp.where(found, slot + 1.0, -float(slots)))
+    low = jnp.floor(jnp.min(jnp.minimum(lows[0], lows[1]), axis=1, keepdims=True) * (1.0 / STEP))
     high = jnp.max(jnp.maximum(highs[0], highs[1]), axis=1, keepdims=True)
-    low = (low.astype(jnp.int32) // STEP) * STEP
-    rounds = (jnp.max(high.astype(jnp.int32) - low) + (STEP - 1)) // STEP
-    firsts = [jnp.max(low[b : b + 1, :]) for b in range(BUCKETS)]
+    rounds = (jnp.max(high - low * STEP).astype(jnp.int32) + (STEP - 1)) // STEP
+    low = jnp.minimum(low, float(slots // STEP)) + float(slots // 2 // STEP)
+    index = lax.broadcasted_iota(jnp.int32, (BUCKETS, 1), 0)
+    weight = jnp.where(
+        index % 4 == 0, 1.0, jnp.where(index % 4 == 1, 64.0, jnp.where(index % 4 == 2, 4096.0, 262144.0))
+    )
+    firsts = []
+    for part in (0, 1):
+        packed = jnp.sum(jnp.where(index // 4 == part, low * weight, 0.0)).astype(jnp.int32)
+        firsts += [(packed >> (6 * n)) & 63 for n in range(4)]
     total_ref[...] = jnp.zeros_like(total_ref)
     x_ids = lax.broadcasted_iota(jnp.int32, (span, 128), 0).astype(bf16)
     l_ids = [
@@ -379,8 +398,9 @@
     def step(t, carry):
         for b in range(BUCKETS):
             half, group = b // GROUPS, b % GROUPS
-            first = pl.multiple_of(jnp.minimum(firsts[b] + t * STEP, slots), STEP)
-            rows = pl.ds(first, STEP)
+            share = b * (slots // BUCKETS // STEP) - slots // 2 // STEP
+            first = ((firsts[b] + share + t) & (slots // STEP - 1)) * STEP
+            rows = pl.ds(pl.multiple_of(first, STEP), STEP)
             x_rows, l_rows = x_ref[half, rows, :], l_ref[rows, :]
             value_rows = [value_ref[c, rows, :] for c in range(8)]
             sums = None
@@ -400,11 +420,8 @@
         return carry
 
     lax.fori_loop(0, rounds, step, 0)
-    for c in range(5):
-        rate = rate_ref[c]
-        if c == 0:
-            out_ref[c] = rate
-            continue
+    copies = []
+    for c in range(1, 5):
         for half in range(HALVES):
             parts = [
                 total_ref[half * GROUPS + g, (c - 1) * lines : c * lines, :]
@@ -413,7 +430,12 @@
             ]
             deposit = jnp.concatenate(parts, axis=0).T
             here = slice(half * span, (half + 1) * span)
-            out_ref[c, here] = rate[here] - deposit
+            done_ref[c - 1, here] = rate_ref[c, here] - deposit
+        copies.append(pltpu.make_async_copy(done_ref.at[c - 1], out_ref.at[c], sems.at[c]))
+        copies[-1].start()
+    for copy in copies:
+        copy.wait()
+    mass_copy.wait()
 
 
 def along(block, distance):
@@ -468,11 +490,15 @@
         name="bin",
         compiler_params=pltpu.CompilerParams(vmem_limit_bytes=20 << 20),
         out_shape=jax.ShapeDtypeStruct((5, cells, lines), f32),
+        in_specs=[pl.BlockSpec(memory_space=pltpu.VMEM)] * 2,
+        out_specs=pl.BlockSpec(memory_space=pltpu.HBM),
         scratch_shapes=[
-            pltpu.VMEM((HALVES, 256 + 2 * STEP, 128), f32),
-            pltpu.VMEM((256 + 2 * STEP, 128), f32),
-            pltpu.VMEM((8, 256 + 2 * STEP, 128), f32),
+            pltpu.VMEM((HALVES, 256, 128), f32),
+            pltpu.VMEM((256, 128), f32),
+            pltpu.VMEM((8, 256, 128), f32),
             pltpu.VMEM((BUCKETS, 8 * lines // GROUPS, cells // HALVES), f32),
+            pltpu.VMEM((4, cells, lines), f32),
+            pltpu.SemaphoreType.DMA((5,)),
         ],
     )(arrived, rate)
 

time: 50.8 us -> 47.4 us (0.933)
  the two profiles are of different devices: /device:TPU:11 before, /device:TPU:3 now
where the time goes in v3:
time: 47.4 us; the launch traced here: 47 us
  Pallas kernels  25.3 us (53%)
  starting transfers between devices  15.1 us (32%)
  waiting for transfers between devices  6.41 us (14%)
    pallas_call x1, Pallas kernels, run_fill(): pl.pallas_call(fill_kernel, name='fill', compiler_params=pltpu.CompilerPa...  11.1 us
    all_to_all x1, starting transfers between devices, body(): lax.all_to_all(outgoing.reshape(peers, 5, 2, 128), ('line', 'slab'), spli...  10.8 us
    pallas_call x1, Pallas kernels, run_bin(): pl.pallas_call(bin_kernel, name='bin', compiler_params=pltpu.CompilerPara...  10.8 us
    ppermute x4, waiting for transfers between devices, along(): lax.ppermute(block, 'line', [(i, (i + distance) % count) for i in range(c...  5.39 us
    ppermute x4, starting transfers between devices, along(): lax.ppermute(block, 'line', [(i, (i + distance) % count) for i in range(c...  4.29 us
    pallas_call x1, Pallas kernels, body(): pl.pallas_call(flux_kernel, name='flux', compiler_params=pltpu.CompilerPa...  1.71 us
    pallas_call x1, Pallas kernels, body(): pl.pallas_call(edge_kernel, name='edge', compiler_params=pltpu.CompilerPa...  1.7 us
    all_to_all x1, waiting for transfers between devices, body(): lax.all_to_all(outgoing.reshape(peers, 5, 2, 128), ('line', 'slab'), spli...  1.02 us
  transfers between devices with their start and end apart: 5, of which 2 were waited for; matrix products, arithmetic and copies ran while one was open for 0% of the time, Pallas kernels for 7%

profile of v3, /device:TPU:3, one launch (start us, length us, event | category | flops | bytes accessed | tf_op | source)
XLA Modules:
  0.0 47.0 jit_solution(11796091355171411282)
XLA Ops:
  0.0 0.0 copy-start.3
  0.0 0.0 copy-start.4
  0.0 0.0 copy-start.6
  0.0 11.1 %fill.1 = f32[1280,128]{1,0:T(8,128)} custom-call(s32[64,128]{1,0:T(8,128)} %bitcast.8, s32[64,128]{1,0:T(8,128)} %bitcast.9, s32[1,8192]{1,0:T(1,128)} %bitcast.10, f32[3,8192]{1,0:T(4,128)} %refs_3_.1, f32[3,8192]{1,0:T(4,128)} %refs_4_.1, f32[2,8192]{1,0:T(2,128)} %refs_5_.1, f32[1,8192]{1,0:T(1,128)} %bitcast.11), custom_call_target="tpu_custom_call" | custom-call | flops 12000000000 | bytes 1000000 | tf_op jit(solution)/shard_map/fill/pallas_call | solution.py:452
  11.2 0.0 copy-start
  11.2 0.0 copy-start.1
  11.2 0.0 copy-start.2
  11.2 10.8 %all-to-all-start = ((f32[128,5,2,128]{3,2,1,0:T(2,128)}), f32[128,5,2,128]{3,2,1,0:T(2,128)S(1)}, u32[]{:S(2)}, u32[]{:S(2)}) async-start(f32[128,5,2,128]{3,2,1,0:T(2,128)} %bitcast.7), calls=%async_computation | async-start | bytes 1310720 | tf_op jit(solution)/shard_map/all_to_all | solution.py:525
  22.0 0.0 copy-done.3
  22.0 0.0 copy-done.4
  22.0 0.0 copy-done.6
  22.0 0.0 copy-done
  22.1 0.0 copy-done.1
  22.1 0.0 copy-done.2
  22.1 0.0 copy-start.5
  22.1 0.0 copy-start.7
  22.1 1.7 %edge.1 = (f32[512,128]{1,0:T(8,128)S(1)}, f32[96,128]{1,0:T(8,128)S(1)}, f32[96,128]{1,0:T(8,128)S(1)}, f32[8,128]{1,0:T(8,128)S(1)}, f32[8,128]{1,0:T(8,128)S(1)}) custom-call(f32[512,128]{1,0:T(8,128)S(1)} %copy-done.1, f32[3,512,128]{2,1,0:T(8,128)S(1)} %copy-done, f32[512,128]{1,0:T(8,128)S(1)} %copy-done.2, f32[512,128]{1,0:T(8,128)S(1)} %copy-done.3, ...), custom_call_target="tpu_custom_call" | custom-call | flops 1000000000 | bytes 2000000 | tf_op jit(solution)/shard_map/edge/pallas_call | solution.py:530
  23.8 1.6 %collective-permute-start = (f32[96,128]{1,0:T(8,128)S(1)}, f32[96,128]{1,0:T(8,128)S(1)}, u32[]{:S(2)}, u32[]{:S(2)}) collective-permute-start(f32[96,128]{1,0:T(8,128)S(1)} %get-tuple-element.11.up_ref), channel_id=1, source_target_pairs={{0,16},{16,32},{32,48},{48,64},{64,80},{80,96},{96,112},{112,0},{1... | collective-permute-start | bytes 147464 | tf_op jit(solution)/shard_map/ppermute | solution.py:443
  25.4 0.0 collective-permute-start.1
  25.4 1.5 %collective-permute-start.2 = (f32[8,128]{1,0:T(8,128)S(1)}, f32[8,128]{1,0:T(8,128)S(1)}, u32[]{:S(2)}, u32[]{:S(2)}) collective-permute-start(f32[8,128]{1,0:T(8,128)S(1)} %get-tuple-element.13), channel_id=1, source_target_pairs={{0,32},{16,48},{32,64},{48,80},{64,96},{80,112},{96,0},{112,16},{1... | collective-permute-start | bytes 12296 | tf_op jit(solution)/shard_map/ppermute | solution.py:443
  26.9 1.2 %collective-permute-start.3 = (f32[8,128]{1,0:T(8,128)S(1)}, f32[8,128]{1,0:T(8,128)S(1)}, u32[]{:S(2)}, u32[]{:S(2)}) collective-permute-start(f32[8,128]{1,0:T(8,128)S(1)} %get-tuple-element.14), channel_id=1, source_target_pairs={{0,96},{16,112},{32,0},{48,16},{64,32},{80,48},{96,64},{112,80},{1... | collective-permute-start | bytes 12296 | tf_op jit(solution)/shard_map/ppermute | solution.py:443
  28.1 5.4 %collective-permute-done.2.far_left_ref = f32[8,128]{1,0:T(8,128)S(1)} collective-permute-done((f32[8,128]{1,0:T(8,128)S(1)}, f32[8,128]{1,0:T(8,128)S(1)}, u32[]{:S(2)}, u32[]{:S(2)}) %collective-permute-start.2) | collective-permute-done | bytes 4128 | tf_op jit(solution)/shard_map/ppermute | solution.py:443
  33.5 0.0 collective-permute-done.3.far_right_ref
  33.5 0.0 collective-permute-done.left_ref
  33.5 0.0 collective-permute-done.1.right_ref
  33.5 0.0 copy-done.5
  33.5 0.0 copy-done.7
  33.5 1.7 %flux.1.rate_ref = f32[5,512,128]{2,1,0:T(8,128)S(1)} custom-call(f32[512,128]{1,0:T(8,128)S(1)} %copy-done.1, f32[3,512,128]{2,1,0:T(8,128)S(1)} %copy-done, f32[512,128]{1,0:T(8,128)S(1)} %copy-done.2, f32[512,128]{1,0:T(8,128)S(1)} %copy-done.3, f32[512,128]{1,0:T(8,128)S(1)} %get-tuple-element.10.own_ref, f32[96,128]{1,0:T(8,128)S(1)} %get-tuple-element.11.up_ref, ...), custom_call_target="tpu_custom_call" | custom-call | flops 2000000000 | bytes 4000000 | tf_op jit(solution)/shard_map/flux/pallas_call | solution.py:545
  35.2 1.0 %all-to-all-done = f32[128,5,2,128]{3,2,1,0:T(2,128)S(1)} async-done(((f32[128,5,2,128]{3,2,1,0:T(2,128)}), f32[128,5,2,128]{3,2,1,0:T(2,128)S(1)}, u32[]{:S(2)}, u32[]{:S(2)}) %all-to-all-start) | async-done | bytes 655392 | tf_op jit(solution)/shard_map/all_to_all | solution.py:525
  36.2 10.8 %bin.1 = f32[5,512,128]{2,1,0:T(8,128)} custom-call(f32[1280,128]{1,0:T(8,128)S(1)} %bitcast.6, f32[5,512,128]{2,1,0:T(8,128)S(1)} %flux.1.rate_ref), custom_call_target="tpu_custom_call" | custom-call | tf_op jit(solution)/shard_map/bin/pallas_call | solution.py:488
Async XLA Ops:
  0.0 22.0 %copy-start.3 = (f32[512,128]{1,0:T(8,128)S(1)}, f32[512,128]{1,0:T(8,128)}, u32[]{:S(2)}) copy-start(f32[512,128]{1,0:T(8,128)} %damp_ref.3) | copy-start | bytes 786436
  0.0 22.0 %copy-start.4 = (bf16[896,256]{1,0:T(8,128)(2,1)S(1)}, bf16[896,256]{1,0:T(8,128)(2,1)}, u32[]{:S(2)}) copy-start(bf16[896,256]{1,0:T(8,128)(2,1)} %constant.6.clone.block_ref) | copy-start | bytes 1376260
  0.0 22.0 %copy-start.6 = (bf16[64,1536]{1,0:T(8,128)(2,1)S(1)}, bf16[64,1536]{1,0:T(8,128)(2,1)}, u32[]{:S(2)}) copy-start(bf16[64,1536]{1,0:T(8,128)(2,1)} %constant.7.clone.probe_ref) | copy-start | bytes 589828
  11.2 10.9 %copy-start = (f32[3,512,128]{2,1,0:T(8,128)S(1)}, f32[3,512,128]{2,1,0:T(8,128)}, u32[]{:S(2)}) copy-start(f32[3,512,128]{2,1,0:T(8,128)} %vel_ref.3) | copy-start | bytes 2359300
  11.2 10.9 %copy-start.1 = (f32[512,128]{1,0:T(8,128)S(1)}, f32[512,128]{1,0:T(8,128)}, u32[]{:S(2)}) copy-start(f32[512,128]{1,0:T(8,128)} %rho_ref.3) | copy-start | bytes 786436
  11.2 10.9 %copy-start.2 = (f32[512,128]{1,0:T(8,128)S(1)}, f32[512,128]{1,0:T(8,128)}, u32[]{:S(2)}) copy-start(f32[512,128]{1,0:T(8,128)} %thrust_ref.3) | copy-start | bytes 786436
  11.2 25.1 %all-to-all-start = ((f32[128,5,2,128]{3,2,1,0:T(2,128)}), f32[128,5,2,128]{3,2,1,0:T(2,128)S(1)}, u32[]{:S(2)}, u32[]{:S(2)}) async-start(f32[128,5,2,128]{3,2,1,0:T(2,128)} %bitcast.7), calls=%async_computation | async-start | bytes 1310720 | tf_op jit(solution)/shard_map/all_to_all | solution.py:525
  22.1 11.4 %copy-start.5 = (bf16[896,256]{1,0:T(8,128)(2,1)S(1)}, bf16[896,256]{1,0:T(8,128)(2,1)}, u32[]{:S(2)}) copy-start(bf16[896,256]{1,0:T(8,128)(2,1)} %constant.6.clone.block_ref) | copy-start | bytes 1376260
  22.1 11.4 %copy-start.7 = (bf16[512,48]{1,0:T(8,128)(2,1)S(1)}, bf16[512,48]{1,0:T(8,128)(2,1)}, u32[]{:S(2)}) copy-start(bf16[512,48]{1,0:T(8,128)(2,1)} %constant.8.clone.fix_ref) | copy-start | bytes 147460
  23.8 9.7 %collective-permute-start = (f32[96,128]{1,0:T(8,128)S(1)}, f32[96,128]{1,0:T(8,128)S(1)}, u32[]{:S(2)}, u32[]{:S(2)}) collective-permute-start(f32[96,128]{1,0:T(8,128)S(1)} %get-tuple-element.11.up_ref), channel_id=1, source_target_pairs={{0,16},{16,32},{32,48},{48,64},{64,80},{80,96},{96,112},{112,0},{1... | collective-permute-start | bytes 147464 | tf_op jit(solution)/shard_map/ppermute | solution.py:443
  25.4 8.1 %collective-permute-start.1 = (f32[96,128]{1,0:T(8,128)S(1)}, f32[96,128]{1,0:T(8,128)S(1)}, u32[]{:S(2)}, u32[]{:S(2)}) collective-permute-start(f32[96,128]{1,0:T(8,128)S(1)} %get-tuple-element.12.down_ref), channel_id=1, source_target_pairs={{0,112},{16,0},{32,16},{48,32},{64,48},{80,64},{96,80},{112,96},{1... | collective-permute-start | bytes 147464 | tf_op jit(solution)/shard_map/ppermute | solution.py:443
  25.4 8.1 %collective-permute-start.2 = (f32[8,128]{1,0:T(8,128)S(1)}, f32[8,128]{1,0:T(8,128)S(1)}, u32[]{:S(2)}, u32[]{:S(2)}) collective-permute-start(f32[8,128]{1,0:T(8,128)S(1)} %get-tuple-element.13), channel_id=1, source_target_pairs={{0,32},{16,48},{32,64},{48,80},{64,96},{80,112},{96,0},{112,16},{1... | collective-permute-start | bytes 12296 | tf_op jit(solution)/shard_map/ppermute | solution.py:443
  26.9 6.6 %collective-permute-start.3 = (f32[8,128]{1,0:T(8,128)S(1)}, f32[8,128]{1,0:T(8,128)S(1)}, u32[]{:S(2)}, u32[]{:S(2)}) collective-permute-start(f32[8,128]{1,0:T(8,128)S(1)} %get-tuple-element.14), channel_id=1, source_target_pairs={{0,96},{16,112},{32,0},{48,16},{64,32},{80,48},{96,64},{112,80},{1... | collective-permute-start | bytes 12296 | tf_op jit(solution)/shard_map/ppermute | solution.py:443
